TPU v7x, 32 devices: a whole 2x2x4 slice. The times are simulated.
32 devices in a mesh: section: 4 (over y, core), seq: 8 (over z, x).
Axes of the slice: x: 2, y: 2, z: 4, core: 2. Of those that a mesh axis runs over, the one named last changes fastest.
Arguments:
- queries: bfloat16 [4, 1024, 2048], P('section', 'seq'), may hold values from -4 to 4
- memory_keys: bfloat16 [4, 1024, 2048], P('section', 'seq'), may hold values from -2.5 to 2.5
- memory_values: bfloat16 [4, 1024, 2048], P('section', 'seq'), may hold values from -4 to 4
- upstream: bfloat16 [4, 1024, 2048], P('section', 'seq'), may hold values from -4 to 4
- inner_rate: float32 [4, 32], P('section'), may hold values from 0.02 to 0.2
- checkpoints: float32 [4, 8, 32, 4096], P('section', 'seq'), may hold values from -0.75 to 0.75
Outputs:
- grad_queries: bfloat16 [4, 1024, 2048], P('section', 'seq')
- grad_keys: bfloat16 [4, 1024, 2048], P('section', 'seq')
- grad_values: bfloat16 [4, 1024, 2048], P('section', 'seq')
- adjoint_start: float32 [4, 8, 32, 4096], P('section', 'seq')
All inputs are finite; a program needn't handle non-finite values.
Results may differ from a plain program's by a relative error of at most 0.001.
Values may be sent and summed in bfloat16 or wider, within the bound.
A program may use at most 128 MiB of HBM per device.

v0:
```python
from functools import partial

import jax
import jax.numpy as jnp
from jax import lax
from jax.sharding import PartitionSpec as P

MB = 64


inner_product = partial(jnp.einsum, precision=lax.Precision.HIGHEST)


def passed_along(block, axis, distance):
    devices = range(lax.axis_size(axis))
    route = [((i - distance) % len(devices), i) for i in devices]
    return lax.ppermute(block, axis, route)


def shifted(value, axis, steps):
    count = lax.axis_size(axis)
    initial, last = (max(0, -steps), min(count, count - steps))
    return lax.ppermute(value, axis, [(source, source + steps) for source in range(initial, last)])


def lower_mask(length):
    row_index = lax.broadcasted_iota(jnp.int32, (length, length), 0)
    col_index = lax.broadcasted_iota(jnp.int32, (length, length), 1)
    return (row_index >= col_index).astype(jnp.float32)


def per_device(queries, memory_keys, memory_values, upstream, inner_rate, checkpoints):
    head_count = inner_rate.shape[1]
    feature_count = queries.shape[2]
    head_size = feature_count // head_count
    tokens = queries.shape[1]
    block_count = tokens // MB

    def to_blocks(array):
        shaped = array[0].astype(jnp.float32).reshape(block_count, MB, head_count, head_size)
        return jnp.transpose(shaped, (0, 2, 1, 3))

    def from_blocks(array):
        return (
            jnp.transpose(array, (0, 2, 1, 3))
            .reshape(1, tokens, feature_count)
            .astype(jnp.bfloat16)
        )

    update_rate = (inner_rate[0] / MB)[:, None, None]
    masked_scores = lower_mask(MB)
    initial = checkpoints[0, 0].reshape(head_count, head_size, head_size)
    key_blocks = to_blocks(memory_keys)
    value_blocks = to_blocks(memory_values)

    def forward(weight_stack, operands):
        current_key, current_value = operands
        error_rows = inner_product("ick,iku->icu", current_key, weight_stack) - current_value
        updated_weight = weight_stack - update_rate * inner_product(
            "fwl,fwn->fln", current_key, error_rows
        )
        return (updated_weight, (weight_stack, error_rows))

    weight_trail, error_trail = lax.scan(forward, initial, (key_blocks, value_blocks))[1]
    cotangent = passed_along(upstream, "section", -1)
    query_blocks = to_blocks(queries)
    grad_blocks = to_blocks(cotangent)
    identity_map = jnp.broadcast_to(
        jnp.eye(head_size, dtype=jnp.float32), (head_count, head_size, head_size)
    )
    empty = jnp.zeros((head_count, head_size, head_size), jnp.float32)

    def compose(stacked, operands):
        current_query, current_key, current_gradient = operands
        attention_scores = inner_product("sxi,sbi->sxb", current_query, current_key) * masked_scores
        carried = inner_product("hmn,hme->hne", attention_scores, current_gradient)
        source_weight = inner_product(
            "fwl,fwn->fln", current_query, current_gradient
        ) - update_rate * inner_product("wik,wiy->wky", current_key, carried)
        projected = inner_product("hnd,hde->hne", current_key, stacked)
        stacked = stacked - update_rate * inner_product("wik,wiy->wky", current_key, projected)
        stacked = stacked + jnp.concatenate([empty, source_weight], axis=2)
        return (stacked, (carried, source_weight))

    stacked, (carried_trail, source_trail) = lax.scan(
        compose,
        jnp.concatenate([identity_map, empty], axis=2),
        (query_blocks, key_blocks, grad_blocks),
        reverse=True,
    )
    linear = stacked[:, :, :head_size]
    offset = stacked[:, :, head_size:]
    shard_count = lax.axis_size("seq")

    def advance(position, adjoint_end):
        shard_begin = inner_product("hde,hef->hdf", linear, adjoint_end) + offset
        return shifted(shard_begin, "seq", -1)

    adjoint_end = lax.fori_loop(0, shard_count - 1, advance, empty)

    def backward(adjoint_carry, operands):
        (
            current_query,
            current_key,
            current_gradient,
            current_weight,
            error_now,
            carried,
            source_weight,
        ) = operands
        projected = inner_product("hnd,hde->hne", current_key, adjoint_carry)
        error_gradient = -update_rate * (carried + projected)
        score_gradient = (
            -update_rate
            * inner_product("hme,hne->hmn", current_gradient, error_now)
            * masked_scores
        )
        query_gradient = inner_product(
            "nyv,nxv->nyx", current_gradient, current_weight
        ) + inner_product("clo,coq->clq", score_gradient, current_key)
        grad_key = (
            inner_product("hne,hde->hnd", error_gradient, current_weight)
            - update_rate * inner_product("hne,hde->hnd", error_now, adjoint_carry)
            + inner_product("fbw,fbe->fwe", score_gradient, current_query)
        )
        previous_weight = (
            adjoint_carry
            + source_weight
            - update_rate * inner_product("wik,wiy->wky", current_key, projected)
        )
        return (previous_weight, (query_gradient, grad_key, -error_gradient))

    shard_start, (query_grads, key_grads, value_grads) = lax.scan(
        backward,
        adjoint_end,
        (
            query_blocks,
            key_blocks,
            grad_blocks,
            weight_trail,
            error_trail,
            carried_trail,
            source_trail,
        ),
        reverse=True,
    )
    adjoint_start = shard_start.reshape(1, 1, head_count, head_size * head_size)
    return (
        from_blocks(query_grads),
        from_blocks(key_grads),
        from_blocks(value_grads),
        adjoint_start,
    )


def solution(mesh):
    return jax.shard_map(
        per_device,
        mesh=mesh,
        in_specs=(
            P("section", "seq", None),
            P("section", "seq", None),
            P("section", "seq", None),
            P("section", "seq", None),
            P("section", None),
            P("section", "seq", None, None),
        ),
        out_specs=(
            P("section", "seq", None),
            P("section", "seq", None),
            P("section", "seq", None),
            P("section", "seq", None, None),
        ),
        check_vma=False,
    )
```

profile of v0, /device:TPU:22, one launch (start us, length us, event | category | flops | bytes accessed | tf_op | source)
XLA Modules:
  0.0 350.6 jit_solution(12833701729509051996)
XLA Ops:
  1.4 3.0 reshape.92
  4.4 2.9 copy.26
  7.2 2.3 reshape.95
  14.2 11.6 %while.65 = (s32[]{:T(128)}, f32[32,64,64]{2,1,0:T(8,128)S(1)}, f32[2,32,64,64]{3,2,1,0:T(8,128)}, f32[2,32,64,64]{3,2,1,0:T(8,128)}, f32[32,1,1]{0,2,1:T(1,128)...) while((s32[]{:T(128)}, f32[32,64,64]{2,1,0:T(8,128)S(1)}, ...), condition=%wide.region_5.6_spmd, body=%wide.region_4.5_spmd.sunk | while | flops 201719808 | bytes 28837584 | solution.py:64
  18.0 2.0 fusion.132
  23.8 2.0 fusion.132
  28.3 2.3 reshape.93
  31.9 3.0 reshape.94
  34.9 4.1 %copy.23 = f32[2,32,64,64]{3,2,1,0:T(8,128)} copy(f32[2,32,64,64]{3,1,2,0:T(8,128)} %bitcast.231) | data formatting | bytes 2097152
  42.3 41.2 %while.66 = (s32[]{:T(128)}, f32[32,64,128]{2,1,0:T(8,128)}, f32[2,32,64,64]{3,2,1,0:T(8,128)}, f32[2,32,64,64]{3,2,1,0:T(8,128)}, f32[32,1,1]{0,2,1:T(1,128)S(1...) while((s32[]{:T(128)}, f32[32,64,128]{2,1,0:T(8,128)}, ...), condition=%wide.region_1.2_spmd.clone, body=%wide.region_0.1_spmd.clone.sunk | while | flops 806494208 | bytes 47220636 | solution.py:85
  42.6 3.0 constant_dynamic-slice_fusion.8
  47.4 2.8 copy.48
  50.2 3.2 convolution_multiply_fusion.8
  53.4 2.3 bitcast_dynamic-update-slice_fusion.12
  63.1 3.0 constant_dynamic-slice_fusion.8
  67.9 2.8 copy.48
  70.7 3.2 convolution_multiply_fusion.8
  73.9 2.2 bitcast_dynamic-update-slice_fusion.12
  83.5 3.2 fusion.71
  86.9 207.6 %while.64 = (s32[]{:T(128)}, f32[32,64,64]{2,1,0:T(8,128)S(1)}, f32[32,64,64]{2,1,0:T(8,128)}, f32[32,64,64]{2,1,0:T(8,128)}, s32[]{:T(128)}) while((s32[]{:T(128)}, f32[32,64,64]{2,1,0:T(8,128)S(1)}, f32[32,64,64]{2,1,0:T(8,128)}, f32[32,64,64]{2,1,0:T(8,128)}, s32[]{:T(128)}) %tuple.124), condition=%wide.region_3.4_spmd, body=%wide.region_2.3_spmd.sunk | while | flops 100794368 | bytes 4194405 | solution.py:99
  86.9 3.7 %convolution_add_fusion.4 = f32[32,64,64]{2,1,0:T(8,128)} fusion(f32[32,64,64]{2,1,0:T(8,128)} %get-tuple-element.973, f32[32,64,64]{2,1,0:T(8,128)} %get-tuple-element.972, f32[32,64,64]{2,1,0:T(8,128)S(1)} %get-tuple-element.966), kind=kOutput, calls=%fused_computation.2.clone.1 | convolution fusion | flops 100794368 | bytes 2097152 | tf_op jit(solution)/shard_map/while/body/eval_jaxpr/hde,hef->hdf/dot_general | solution.py:96
  90.5 2.4 collective-permute-start
  93.0 26.1 %collective-permute-done = f32[32,64,64]{2,1,0:T(8,128)S(1)} collective-permute-done((f32[32,64,64]{2,1,0:T(8,128)}, f32[32,64,64]{2,1,0:T(8,128)S(1)}, u32[]{:S(2)}, u32[]{:S(2)}) %collective-permute-start) | collective-permute-done | bytes 524320 | tf_op jit(solution)/shard_map/while/body/eval_jaxpr/ppermute | solution.py:23
  119.1 3.7 %convolution_add_fusion.4 = f32[32,64,64]{2,1,0:T(8,128)} fusion(f32[32,64,64]{2,1,0:T(8,128)} %get-tuple-element.973, f32[32,64,64]{2,1,0:T(8,128)} %get-tuple-element.972, f32[32,64,64]{2,1,0:T(8,128)S(1)} %get-tuple-element.966), kind=kOutput, calls=%fused_computation.2.clone.1 | convolution fusion | flops 100794368 | bytes 2097152 | tf_op jit(solution)/shard_map/while/body/eval_jaxpr/hde,hef->hdf/dot_general | solution.py:96
  122.8 1.9 collective-permute-start
  124.7 25.8 %collective-permute-done = f32[32,64,64]{2,1,0:T(8,128)S(1)} collective-permute-done((f32[32,64,64]{2,1,0:T(8,128)}, f32[32,64,64]{2,1,0:T(8,128)S(1)}, u32[]{:S(2)}, u32[]{:S(2)}) %collective-permute-start) | collective-permute-done | bytes 524320 | tf_op jit(solution)/shard_map/while/body/eval_jaxpr/ppermute | solution.py:23
  150.4 3.7 %convolution_add_fusion.4 = f32[32,64,64]{2,1,0:T(8,128)} fusion(f32[32,64,64]{2,1,0:T(8,128)} %get-tuple-element.973, f32[32,64,64]{2,1,0:T(8,128)} %get-tuple-element.972, f32[32,64,64]{2,1,0:T(8,128)S(1)} %get-tuple-element.966), kind=kOutput, calls=%fused_computation.2.clone.1 | convolution fusion | flops 100794368 | bytes 2097152 | tf_op jit(solution)/shard_map/while/body/eval_jaxpr/hde,hef->hdf/dot_general | solution.py:96
  154.1 1.9 collective-permute-start
  156.0 24.9 %collective-permute-done = f32[32,64,64]{2,1,0:T(8,128)S(1)} collective-permute-done((f32[32,64,64]{2,1,0:T(8,128)}, f32[32,64,64]{2,1,0:T(8,128)S(1)}, u32[]{:S(2)}, u32[]{:S(2)}) %collective-permute-start) | collective-permute-done | bytes 524320 | tf_op jit(solution)/shard_map/while/body/eval_jaxpr/ppermute | solution.py:23
  181.0 3.7 %convolution_add_fusion.4 = f32[32,64,64]{2,1,0:T(8,128)} fusion(f32[32,64,64]{2,1,0:T(8,128)} %get-tuple-element.973, f32[32,64,64]{2,1,0:T(8,128)} %get-tuple-element.972, f32[32,64,64]{2,1,0:T(8,128)S(1)} %get-tuple-element.966), kind=kOutput, calls=%fused_computation.2.clone.1 | convolution fusion | flops 100794368 | bytes 2097152 | tf_op jit(solution)/shard_map/while/body/eval_jaxpr/hde,hef->hdf/dot_general | solution.py:96
  186.5 24.1 %collective-permute-done = f32[32,64,64]{2,1,0:T(8,128)S(1)} collective-permute-done((f32[32,64,64]{2,1,0:T(8,128)}, f32[32,64,64]{2,1,0:T(8,128)S(1)}, u32[]{:S(2)}, u32[]{:S(2)}) %collective-permute-start) | collective-permute-done | bytes 524320 | tf_op jit(solution)/shard_map/while/body/eval_jaxpr/ppermute | solution.py:23
  210.6 3.7 %convolution_add_fusion.4 = f32[32,64,64]{2,1,0:T(8,128)} fusion(f32[32,64,64]{2,1,0:T(8,128)} %get-tuple-element.973, f32[32,64,64]{2,1,0:T(8,128)} %get-tuple-element.972, f32[32,64,64]{2,1,0:T(8,128)S(1)} %get-tuple-element.966), kind=kOutput, calls=%fused_computation.2.clone.1 | convolution fusion | flops 100794368 | bytes 2097152 | tf_op jit(solution)/shard_map/while/body/eval_jaxpr/hde,hef->hdf/dot_general | solution.py:96
  216.2 23.2 %collective-permute-done = f32[32,64,64]{2,1,0:T(8,128)S(1)} collective-permute-done((f32[32,64,64]{2,1,0:T(8,128)}, f32[32,64,64]{2,1,0:T(8,128)S(1)}, u32[]{:S(2)}, u32[]{:S(2)}) %collective-permute-start) | collective-permute-done | bytes 524320 | tf_op jit(solution)/shard_map/while/body/eval_jaxpr/ppermute | solution.py:23
  239.4 3.7 %convolution_add_fusion.4 = f32[32,64,64]{2,1,0:T(8,128)} fusion(f32[32,64,64]{2,1,0:T(8,128)} %get-tuple-element.973, f32[32,64,64]{2,1,0:T(8,128)} %get-tuple-element.972, f32[32,64,64]{2,1,0:T(8,128)S(1)} %get-tuple-element.966), kind=kOutput, calls=%fused_computation.2.clone.1 | convolution fusion | flops 100794368 | bytes 2097152 | tf_op jit(solution)/shard_map/while/body/eval_jaxpr/hde,hef->hdf/dot_general | solution.py:96
  245.0 22.4 %collective-permute-done = f32[32,64,64]{2,1,0:T(8,128)S(1)} collective-permute-done((f32[32,64,64]{2,1,0:T(8,128)}, f32[32,64,64]{2,1,0:T(8,128)S(1)}, u32[]{:S(2)}, u32[]{:S(2)}) %collective-permute-start) | collective-permute-done | bytes 524320 | tf_op jit(solution)/shard_map/while/body/eval_jaxpr/ppermute | solution.py:23
  267.3 3.7 %convolution_add_fusion.4 = f32[32,64,64]{2,1,0:T(8,128)} fusion(f32[32,64,64]{2,1,0:T(8,128)} %get-tuple-element.973, f32[32,64,64]{2,1,0:T(8,128)} %get-tuple-element.972, f32[32,64,64]{2,1,0:T(8,128)S(1)} %get-tuple-element.966), kind=kOutput, calls=%fused_computation.2.clone.1 | convolution fusion | flops 100794368 | bytes 2097152 | tf_op jit(solution)/shard_map/while/body/eval_jaxpr/hde,hef->hdf/dot_general | solution.py:96
  272.9 21.5 %collective-permute-done = f32[32,64,64]{2,1,0:T(8,128)S(1)} collective-permute-done((f32[32,64,64]{2,1,0:T(8,128)}, f32[32,64,64]{2,1,0:T(8,128)S(1)}, u32[]{:S(2)}, u32[]{:S(2)}) %collective-permute-start) | collective-permute-done | bytes 524320 | tf_op jit(solution)/shard_map/while/body/eval_jaxpr/ppermute | solution.py:23
  294.4 44.5 %while.67 = (s32[]{:T(128)}, f32[32,64,64]{2,1,0:T(8,128)S(1)}, bf16[2,32,64,64]{3,2,1,0:T(8,128)(2,1)}, bf16[2,32,64,64]{3,2,1,0:T(8,128)(2,1)}, bf16[2,32,64,6...) while((s32[]{:T(128)}, f32[32,64,64]{2,1,0:T(8,128)S(1)}, ...), condition=%wide.region_7.8_spmd.clone, body=%wide.region_6.7_spmd.clone.sunk | while | flops 807149568 | bytes 63497148 | solution.py:133
  304.3 3.5 bitcast_dynamic-update-slice_fusion.14
  307.7 1.9 fusion.166
  313.5 2.4 fusion.168
  319.4 2.1 fusion.161
  321.5 3.5 bitcast_dynamic-update-slice_fusion.14
  325.0 1.9 fusion.166
  330.7 2.4 fusion.168
  336.6 2.1 fusion.161
  338.9 2.0 copy.29
  344.2 2.7 convert_element_type.90
  (147 shorter events, 66.8 us)
Async XLA Ops:
  0.6 31.2 %collective-permute-start.1 = (bf16[1,128,2048]{2,1,0:T(8,128)(2,1)}, bf16[1,128,2048]{2,1,0:T(8,128)(2,1)}, u32[]{:S(2)}, u32[]{:S(2)}) collective-permute-start(bf16[1,128,2048]{2,1,0:T(8,128)(2,1)} %param.17), channel_id=1, source_target_pairs={{8,0},{16,8},{24,16},{0,24},{9,1},{17,9},{25,17},{1,25},{10,2},{18... | collective-permute-start | bytes 1572872 | tf_op jit(solution)/shard_map/ppermute | solution.py:17
  4.4 2.9 copy-start.23
  14.2 1.9 copy-start.9
  16.1 1.8 copy-start.6
  17.8 2.1 copy-start.10
  18.0 2.0 copy-start.7
  20.0 1.9 copy-start.9
  21.9 1.8 copy-start.6
  23.6 2.1 copy-start.10
  23.8 2.0 copy-start.7
  26.1 2.3 copy-start.24
  50.2 3.2 copy-start
  53.4 2.3 copy-start.2
  55.7 1.6 copy-start.13
  58.6 3.6 %copy-start.14 = (f32[2,32,64,64]{3,2,1,0:T(8,128)}, f32[2,32,64,64]{3,2,1,0:T(8,128)S(1)}, u32[]{:S(2)}) copy-start(f32[2,32,64,64]{3,2,1,0:T(8,128)S(1)} %get-tuple-element.954) | copy-start | bytes 3145732 | tf_op jit(solution)/shard_map/while
  70.7 3.2 copy-start
  73.9 2.2 copy-start.2
  76.1 1.6 copy-start.13
  78.9 3.6 %copy-start.14 = (f32[2,32,64,64]{3,2,1,0:T(8,128)}, f32[2,32,64,64]{3,2,1,0:T(8,128)S(1)}, u32[]{:S(2)}) copy-start(f32[2,32,64,64]{3,2,1,0:T(8,128)S(1)} %get-tuple-element.954) | copy-start | bytes 3145732 | tf_op jit(solution)/shard_map/while
  90.5 28.5 %collective-permute-start = (f32[32,64,64]{2,1,0:T(8,128)}, f32[32,64,64]{2,1,0:T(8,128)S(1)}, u32[]{:S(2)}, u32[]{:S(2)}) collective-permute-start(f32[32,64,64]{2,1,0:T(8,128)} %convolution_add_fusion.4), channel_id=1, source_target_pairs={{1,0},{2,1},{3,2},{4,3},{5,4},{6,5},{7,6},{9,8},{10,9},{11,10},{12... | collective-permute-start | bytes 1572872 | tf_op jit(solution)/shard_map/while/body/eval_jaxpr/ppermute | solution.py:23
  122.8 27.7 %collective-permute-start = (f32[32,64,64]{2,1,0:T(8,128)}, f32[32,64,64]{2,1,0:T(8,128)S(1)}, u32[]{:S(2)}, u32[]{:S(2)}) collective-permute-start(f32[32,64,64]{2,1,0:T(8,128)} %convolution_add_fusion.4), channel_id=1, source_target_pairs={{1,0},{2,1},{3,2},{4,3},{5,4},{6,5},{7,6},{9,8},{10,9},{11,10},{12... | collective-permute-start | bytes 1572872 | tf_op jit(solution)/shard_map/while/body/eval_jaxpr/ppermute | solution.py:23
  154.1 26.8 %collective-permute-start = (f32[32,64,64]{2,1,0:T(8,128)}, f32[32,64,64]{2,1,0:T(8,128)S(1)}, u32[]{:S(2)}, u32[]{:S(2)}) collective-permute-start(f32[32,64,64]{2,1,0:T(8,128)} %convolution_add_fusion.4), channel_id=1, source_target_pairs={{1,0},{2,1},{3,2},{4,3},{5,4},{6,5},{7,6},{9,8},{10,9},{11,10},{12... | collective-permute-start | bytes 1572872 | tf_op jit(solution)/shard_map/while/body/eval_jaxpr/ppermute | solution.py:23
  184.6 26.0 %collective-permute-start = (f32[32,64,64]{2,1,0:T(8,128)}, f32[32,64,64]{2,1,0:T(8,128)S(1)}, u32[]{:S(2)}, u32[]{:S(2)}) collective-permute-start(f32[32,64,64]{2,1,0:T(8,128)} %convolution_add_fusion.4), channel_id=1, source_target_pairs={{1,0},{2,1},{3,2},{4,3},{5,4},{6,5},{7,6},{9,8},{10,9},{11,10},{12... | collective-permute-start | bytes 1572872 | tf_op jit(solution)/shard_map/while/body/eval_jaxpr/ppermute | solution.py:23
  214.3 25.1 %collective-permute-start = (f32[32,64,64]{2,1,0:T(8,128)}, f32[32,64,64]{2,1,0:T(8,128)S(1)}, u32[]{:S(2)}, u32[]{:S(2)}) collective-permute-start(f32[32,64,64]{2,1,0:T(8,128)} %convolution_add_fusion.4), channel_id=1, source_target_pairs={{1,0},{2,1},{3,2},{4,3},{5,4},{6,5},{7,6},{9,8},{10,9},{11,10},{12... | collective-permute-start | bytes 1572872 | tf_op jit(solution)/shard_map/while/body/eval_jaxpr/ppermute | solution.py:23
  243.1 24.3 %collective-permute-start = (f32[32,64,64]{2,1,0:T(8,128)}, f32[32,64,64]{2,1,0:T(8,128)S(1)}, u32[]{:S(2)}, u32[]{:S(2)}) collective-permute-start(f32[32,64,64]{2,1,0:T(8,128)} %convolution_add_fusion.4), channel_id=1, source_target_pairs={{1,0},{2,1},{3,2},{4,3},{5,4},{6,5},{7,6},{9,8},{10,9},{11,10},{12... | collective-permute-start | bytes 1572872 | tf_op jit(solution)/shard_map/while/body/eval_jaxpr/ppermute | solution.py:23
  271.0 23.4 %collective-permute-start = (f32[32,64,64]{2,1,0:T(8,128)}, f32[32,64,64]{2,1,0:T(8,128)S(1)}, u32[]{:S(2)}, u32[]{:S(2)}) collective-permute-start(f32[32,64,64]{2,1,0:T(8,128)} %convolution_add_fusion.4), channel_id=1, source_target_pairs={{1,0},{2,1},{3,2},{4,3},{5,4},{6,5},{7,6},{9,8},{10,9},{11,10},{12... | collective-permute-start | bytes 1572872 | tf_op jit(solution)/shard_map/while/body/eval_jaxpr/ppermute | solution.py:23
  304.2 3.5 copy-start.8
  304.2 3.5 copy-start.12
  307.7 1.9 copy-start.11
  309.7 1.9 copy-start.1
  311.5 1.9 copy-start.5
  311.6 1.9 copy-start.19
  315.9 3.2 copy-start.20
  315.9 1.8 copy-start.17
  317.8 1.6 copy-start.15
  319.2 2.3 copy-start.18
  321.5 3.5 copy-start.8
  321.5 3.5 copy-start.12
  325.0 1.9 copy-start.11
  326.9 1.9 copy-start.1
  328.7 1.9 copy-start.5
  328.8 1.9 copy-start.19
  333.2 3.2 copy-start.20
  333.2 1.8 copy-start.17
  335.0 1.6 copy-start.15
  336.4 2.3 copy-start.18
  338.9 3.6 %copy-start.21 = (bf16[2,32,64,64]{3,2,1,0:T(8,128)(2,1)S(1)}, bf16[2,32,64,64]{3,2,1,0:T(8,128)(2,1)}, u32[]{:S(2)}) copy-start(bf16[2,32,64,64]{3,2,1,0:T(8,128)(2,1)} %get-tuple-element.542) | copy-start | bytes 1572868
  342.5 4.4 %copy-start.22 = (bf16[2,32,64,64]{3,2,1,0:T(8,128)(2,1)S(1)}, bf16[2,32,64,64]{3,2,1,0:T(8,128)(2,1)}, u32[]{:S(2)}) copy-start(bf16[2,32,64,64]{3,2,1,0:T(8,128)(2,1)} %get-tuple-element.543) | copy-start | bytes 1572868
  (6 other events, 7.0 us)
where the time goes:
time: 355 us; the launch traced here: 351 us
  waiting for transfers between devices  168 us (47%)
  matrix products  89.3 us (25%)
  local copies, waits for them, and re-layouts  66.4 us (19%)
  starting transfers between devices  13.9 us (4%)
  loops' own time  11.1 us (3%)
    ppermute x7, waiting for transfers between devices, shifted(): lax.ppermute(value, axis, [(source, source + steps) for source in range(i...  168 us
    dot_general x7, matrix products, advance(): shard_begin = inner_product('hde,hef->hdf', linear, adjoint_end) + offset  25.7 us
    dynamic_slice x10, local copies, waits for them, and re-layouts, per_device(): lax.scan(forward, initial, (key_blocks, value_blocks))[1]  18.2 us
    ppermute x7, starting transfers between devices, shifted(): lax.ppermute(value, axis, [(source, source + steps) for source in range(i...  13.9 us
    transpose x4, local copies, waits for them, and re-layouts, to_blocks(): return jnp.transpose(shaped, (0, 2, 1, 3))  10.6 us
    another operation x1, loops' own time, per_device(): lax.scan(backward, adjoint_end, (query_blocks, key_blocks, grad_blocks, w...  10.4 us
    convert_element_type x6, local copies, waits for them, and re-layouts, from_blocks(): return jnp.transpose(array, (0, 2, 1, 3)).reshape(1, tokens, feature_coun...  10.2 us
    unnamed x16, local copies, waits for them, and re-layouts  9.31 us
  transfers between devices with their start and end apart: 8, of which 7 were waited for; matrix products, arithmetic and copies ran while one was open for 8% of the time, Pallas kernels for 0%

commit v1 on v0

v1 whole, which is shorter than its diff:
```python
from functools import partial

import jax
import jax.numpy as jnp
from jax import lax
from jax.experimental import pallas as pl
from jax.experimental.pallas import tpu as pltpu
from jax.sharding import PartitionSpec as P

MB = 64
LANES = 128
F32 = jnp.float32
BF16 = jnp.bfloat16
MESH = pl.DeviceIdType.MESH


def passed_along(block, axis, distance):
    devices = range(lax.axis_size(axis))
    route = [((i - distance) % len(devices), i) for i in devices]
    return lax.ppermute(block, axis, route)


def nn(a, b):
    return lax.dot_general(a, b, (((1,), (0,)), ((), ())), preferred_element_type=F32)


def nt(a, b):
    return lax.dot_general(a, b, (((1,), (1,)), ((), ())), preferred_element_type=F32)


def tn(a, b):
    return lax.dot_general(a, b, (((0,), (0,)), ((), ())), preferred_element_type=F32)


def split(x):
    high = x.astype(BF16)
    return high, (x - high.astype(F32)).astype(BF16)


def stacked(parts):
    return jnp.concatenate(parts, axis=0)


def tiles(x):
    return [x[:, i : i + LANES] for i in range(0, x.shape[1], LANES)]


def diagonal(x, dh):
    per = LANES // dh
    lane = lax.broadcasted_iota(jnp.int32, (x.shape[0], LANES), 1) // dh
    masks = [(lane == i).astype(F32).astype(BF16) for i in range(per)]
    pieces = tiles(x)
    zero = jnp.zeros((x.shape[0], LANES), x.dtype)
    rows = []
    for t, piece in enumerate(pieces):
        for i in range(per):
            row = [zero] * len(pieces)
            row[t] = piece * masks[i]
            rows.append(jnp.concatenate(row, axis=1))
    return stacked(rows)


def folded(a, b, dh):
    per = LANES // dh
    lane = lax.broadcasted_iota(jnp.int32, (dh, LANES), 1) // dh
    out = []
    for left, right in zip(tiles(a), tiles(b)):
        product = tn(left, right)
        value = product[:dh]
        for i in range(1, per):
            value = jnp.where(lane == i, product[i * dh : (i + 1) * dh], value)
        out.append(value)
    return jnp.concatenate(out, axis=1)


def rows_times(x, weights, multiply=nn):
    high, low = split(x)
    both = multiply(stacked([high, low]), weights)
    return both[: x.shape[0]] + both[x.shape[0] :]


def full_times(x, weights, multiply=nn):
    return rows_times(x, weights[0], multiply) + multiply(x.astype(BF16), weights[1])


def halves(x, dh):
    high, low = split(x)
    return diagonal(high, dh), diagonal(low, dh)


def exact_times(x, weights, multiply=nn):
    return multiply(x, weights[0]) + multiply(x, weights[1])


def doubled(a, b):
    return stacked([a, a]), stacked(split(b))


def lane_index(shape, dh):
    return lax.broadcasted_iota(jnp.int32, shape, 1) % dh


def local_part(q, k, v, z, c, w, dh):
    count = len(q)
    width = c.shape[1]
    row = lax.broadcasted_iota(jnp.int32, (MB, width), 0)
    upper = (lane_index((MB, width), MB) >= row).astype(F32)
    eye = lax.broadcasted_iota(jnp.int32, (dh, width), 0) == lane_index((dh, width), dh)
    weights, errors, carried, key_part, query_grads = [], [], [], [], []
    linear, source = [], []
    for t in range(count):
        whole = halves(w, dh)
        e = exact_times(k[t], whole) - v[t].astype(F32)
        weights.append(w)
        errors.append(e)
        zd = diagonal(z[t], dh)
        qd = diagonal(q[t], dh)
        scores = nt(k[t], qd) * upper
        carry = rows_times(scores, zd)
        score_grad = rows_times(e, zd, nt) * (upper * -c)
        key_part.append(rows_times(score_grad, qd))
        sg_high, sg_low = split(score_grad)
        query_grads.append(
            exact_times(z[t], whole, nt)
            + folded(stacked([sg_high, sg_low]), stacked([k[t], k[t]]), dh)
        )
        carried.append(carry)
        high, low = split(carry * -c)
        source.append(folded(stacked([q[t], k[t], k[t]]), stacked([z[t], high, low]), dh))
        gram = folded(k[t], k[t], dh)
        linear.append(jnp.where(eye, 1.0, 0.0) - c * gram)
        if t + 1 < count:
            w = w - c * folded(*doubled(k[t], e), dh)
    a, b = linear[-1], source[-1]
    for t in range(count - 2, -1, -1):
        b = full_times(linear[t], halves(b, dh)) + source[t]
        a = full_times(linear[t], halves(a, dh))
    return weights, errors, carried, key_part, query_grads, a, b


def final_part(q, k, z, c, weights, errors, carried, key_part, g, dh):
    count = len(q)
    key_grads, value_grads = [None] * count, [None] * count
    for t in range(count - 1, -1, -1):
        whole = halves(g, dh)
        minus = c * (carried[t] + exact_times(k[t], whole))
        value_grads[t] = minus
        key_grads[t] = (
            key_part[t]
            - full_times(minus, halves(weights[t], dh), nt)
            - c * full_times(errors[t], whole, nt)
        )
        high, low = split(-minus)
        g = g + folded(stacked([q[t], k[t], k[t]]), stacked([z[t], high, low]), dh)
    return key_grads, value_grads, g


def cut(ref):
    return [ref[i : i + MB, :] for i in range(0, ref.shape[0], MB)]


def put(ref, parts):
    size = ref.shape[0] // len(parts)
    for i, part in enumerate(parts):
        ref[i * size : (i + 1) * size, :] = part.astype(ref.dtype)


def local_kernel(dh, q, k, v, z, c, w, gq, trail, err, car, kp, a, b):
    weights, errors, carried, key_part, query_grads, linear, offset = local_part(
        cut(q), cut(k), cut(v), cut(z), c[...], w[...], dh
    )
    put(gq, query_grads)
    put(trail, weights)
    put(err, errors)
    put(car, carried)
    put(kp, key_part)
    a[...] = linear
    b[...] = offset


def final_kernel(dh, q, k, z, c, trail, err, car, kp, g, gk, gv, start):
    count = q.shape[0] // MB
    weights = [trail[i * dh : (i + 1) * dh, :] for i in range(count)]
    key_grads, value_grads, first = final_part(
        cut(q), cut(k), cut(z), c[...], weights, cut(err), cut(car), cut(kp), g[...], dh
    )
    put(gk, key_grads)
    put(gv, value_grads)
    start[...] = first


def relay_kernel(dh, width, a, b, end, outgoing, send_sem, recv_sem):
    shard = lax.axis_index("seq")
    section = lax.axis_index("section")
    shards = lax.axis_size("seq")
    chunks = b.shape[1] // width
    before = (section, jnp.maximum(shard - 1, 0))
    after = (section, jnp.minimum(shard + 1, shards - 1))
    not_first = shard > 0
    not_last = shard < shards - 1
    barrier = pltpu.get_barrier_semaphore()

    @pl.when(not_first)
    def _():
        pl.semaphore_signal(barrier, inc=1, device_id=before, device_id_type=MESH)

    @pl.when(not_last)
    def _():
        pl.semaphore_signal(barrier, inc=1, device_id=after, device_id_type=MESH)

    pl.semaphore_wait(barrier, not_first.astype(jnp.int32) + not_last.astype(jnp.int32))

    def copy(i):
        lanes = pl.ds(i * width, width)
        return pltpu.make_async_remote_copy(
            src_ref=outgoing.at[:, lanes],
            dst_ref=end.at[:, lanes],
            send_sem=send_sem.at[i],
            recv_sem=recv_sem.at[i],
            device_id=before,
            device_id_type=MESH,
        )

    for i in range(chunks):
        lanes = pl.ds(i * width, width)

        @pl.when(not_last)
        def _():
            copy(i).wait_recv()
            @pl.when(not_first)
            def _():
                outgoing[:, lanes] = (
                    full_times(a[:, lanes], halves(end[:, lanes], dh)) + b[:, lanes]
                )

        @pl.when(jnp.logical_not(not_last))
        def _():
            end[:, lanes] = jnp.zeros((end.shape[0], width), F32)
            outgoing[:, lanes] = b[:, lanes]

        @pl.when(not_first)
        def _():
            copy(i).start()

    @pl.when(not_first)
    def _():
        for i in range(chunks):
            copy(i).wait_send()


def per_device(queries, memory_keys, memory_values, upstream, inner_rate, checkpoints):
    heads = inner_rate.shape[1]
    features = queries.shape[2]
    dh = features // heads
    tokens = queries.shape[1]
    width = min(2 * LANES, features)
    groups = features // width
    count = tokens // MB

    q, k, v = queries[0], memory_keys[0], memory_values[0]
    z = passed_along(upstream, "section", -1)[0]
    c = jnp.repeat(inner_rate / MB, dh, axis=1)
    initial = checkpoints.reshape(heads, dh, dh).transpose(1, 0, 2).reshape(dh, features)

    def spec(rows):
        return pl.BlockSpec((rows, width), lambda i: (0, i))

    def shape(rows, kind=F32):
        return jax.ShapeDtypeStruct((rows, features), kind)

    gq, trail, err, car, kp, a, b = pl.pallas_call(
        partial(local_kernel, dh),
        grid=(groups,),
        in_specs=[spec(tokens)] * 4 + [spec(1), spec(dh)],
        out_specs=[spec(tokens), spec(count * dh), spec(tokens), spec(tokens), spec(tokens), spec(dh), spec(dh)],
        out_shape=[shape(tokens, BF16), shape(count * dh), shape(tokens), shape(tokens), shape(tokens), shape(dh), shape(dh)],
        name="local_part",
    )(q, k, v, z, c, initial)

    vmem = pl.BlockSpec(memory_space=pltpu.VMEM)
    end = pl.pallas_call(
        partial(relay_kernel, dh, width),
        in_specs=[vmem, vmem],
        out_specs=vmem,
        out_shape=shape(dh),
        scratch_shapes=[
            pltpu.VMEM((dh, features), F32),
            pltpu.SemaphoreType.DMA((groups,)),
            pltpu.SemaphoreType.DMA((groups,)),
        ],
        compiler_params=pltpu.CompilerParams(collective_id=0, has_side_effects=True),
        name="relay",
    )(a, b)

    gk, gv, start = pl.pallas_call(
        partial(final_kernel, dh),
        grid=(groups,),
        in_specs=[spec(tokens)] * 3 + [spec(1), spec(count * dh), spec(tokens), spec(tokens), spec(tokens), spec(dh)],
        out_specs=[spec(tokens), spec(tokens), spec(dh)],
        out_shape=[shape(tokens, BF16), shape(tokens, BF16), shape(dh)],
        name="final_part",
    )(q, k, z, c, trail, err, car, kp, end)
    start = start.reshape(dh, heads, dh).transpose(1, 0, 2).reshape(1, 1, heads, dh * dh)
    return gq[None], gk[None], gv[None], start


def solution(mesh):
    return jax.shard_map(
        per_device,
        mesh=mesh,
        in_specs=(
            P("section", "seq", None),
            P("section", "seq", None),
            P("section", "seq", None),
            P("section", "seq", None),
            P("section", None),
            P("section", "seq", None, None),
        ),
        out_specs=(
            P("section", "seq", None),
            P("section", "seq", None),
            P("section", "seq", None),
            P("section", "seq", None, None),
        ),
        check_vma=False,
    )
```

time: 355 us -> 80.4 us (0.23)
  the two profiles are of different devices: /device:TPU:22 before, /device:TPU:0 now
where the time goes in v1:
time: 80.4 us; the launch traced here: 80 us
  Pallas kernels  65.8 us (82%)
  local copies, waits for them, and re-layouts  7.97 us (10%)
  starting transfers between devices  2.49 us (3%)
  waiting for transfers between devices  2.38 us (3%)
    pallas_call x1, Pallas kernels, per_device(): pl.pallas_call(partial(relay_kernel, dh, width), in_specs=[vmem, vmem], o...  41.2 us
    pallas_call x1, Pallas kernels, per_device(): pl.pallas_call(partial(local_kernel, dh), grid=(groups,), in_specs=[spec(...  14.3 us
    pallas_call x1, Pallas kernels, per_device(): pl.pallas_call(partial(final_kernel, dh), grid=(groups,), in_specs=[spec(...  10.3 us
    reshape x3, local copies, waits for them, and re-layouts, per_device(): checkpoints.reshape(heads, dh, dh).transpose(1, 0, 2).reshape(dh, features)  3.22 us
    reshape x2, local copies, waits for them, and re-layouts, per_device(): start.reshape(dh, heads, dh).transpose(1, 0, 2)  2.6 us
    ppermute x1, starting transfers between devices, passed_along(): return lax.ppermute(block, axis, route)  2.49 us
    ppermute x1, waiting for transfers between devices, passed_along(): return lax.ppermute(block, axis, route)  2.38 us
  transfers between devices with their start and end apart: 1, of which 1 were waited for; matrix products, arithmetic and copies ran while one was open for 6% of the time, Pallas kernels for 0%

profile of v1, /device:TPU:0, one launch (start us, length us, event | category | flops | bytes accessed | tf_op | source)
XLA Modules:
  0.0 80.0 jit_solution(11491475173675970725)
XLA Ops:
  0.6 2.5 %collective-permute-start = (bf16[1,128,2048]{2,1,0:T(8,128)(2,1)}, bf16[1,128,2048]{2,1,0:T(8,128)(2,1)S(1)}, u32[]{:S(2)}, u32[]{:S(2)}) collective-permute-start(bf16[1,128,2048]{2,1,0:T(8,128)(2,1)} %param.9), channel_id=1, source_target_pairs={{8,0},{16,8},{24,16},{0,24},{9,1},{17,9},{25,17},{1,25},{10,2},{18... | collective-permute-start | bytes 1572872 | tf_op jit(solution)/shard_map/ppermute | solution.py:20
  3.1 0.7 multiply_bitcast_fusion
  3.8 0.1 broadcast_in_dim.14
  3.8 0.7 broadcast_in_dim.15.c
  4.5 1.5 %reshape.25 = f32[32,64,64]{2,1,0:T(8,128)S(1)} reshape(f32[1,1,32,4096]{3,2,1,0:T(8,128)} %param.11) | data formatting | bytes 1048576 | tf_op jit(solution)/shard_map/reshape | solution.py:263
  6.0 0.6 copy.13
  6.6 1.2 %reshape.26.w = f32[64,2048]{1,0:T(8,128)} reshape(f32[64,32,64]{2,1,0:T(8,128)S(1)} %bitcast.15) | data formatting | bytes 1048576 | tf_op jit(solution)/shard_map/reshape | solution.py:263
  7.8 2.4 %collective-permute-done = bf16[1,128,2048]{2,1,0:T(8,128)(2,1)S(1)} collective-permute-done((bf16[1,128,2048]{2,1,0:T(8,128)(2,1)}, bf16[1,128,2048]{2,1,0:T(8,128)(2,1)S(1)}, u32[]{:S(2)}, u32[]{:S(2)}) %collective-permute-start) | collective-permute-done | bytes 524320 | tf_op jit(solution)/shard_map/ppermute | solution.py:20
  10.1 0.0 copy-start
  10.1 0.8 copy-done
  10.9 14.3 %local_part.1 = (bf16[128,2048]{1,0:T(8,128)(2,1)}, f32[128,2048]{1,0:T(8,128)}, f32[128,2048]{1,0:T(8,128)}, f32[128,2048]{1,0:T(8,128)}, f32[128,2048]{1,0:T(8...) custom-call(bf16[128,2048]{1,0:T(8,128)(2,1)} %bitcast.17, bf16[128,2048]{1,0:T(8,128)(2,1)} %bitcast.19, ...), custom_call_target="tpu_custom_call" | custom-call | tf_op jit(solution)/shard_map/local_part/pallas_call | solution.py:271
  25.2 41.2 %relay.1.g = f32[64,2048]{1,0:T(8,128)} custom-call(f32[64,2048]{1,0:T(8,128)} %get-tuple-element.19.a, f32[64,2048]{1,0:T(8,128)} %get-tuple-element.20.b), custom_call_target="tpu_custom_call" | custom-call | tf_op jit(solution)/shard_map/relay/pallas_call | solution.py:281
  66.4 10.3 %final_part.1 = (bf16[128,2048]{1,0:T(8,128)(2,1)}, bf16[128,2048]{1,0:T(8,128)(2,1)}, f32[64,2048]{1,0:T(8,128)}) custom-call(bf16[128,2048]{1,0:T(8,128)(2,1)} %bitcast.18, bf16[128,2048]{1,0:T(8,128)(2,1)} %bitcast.20, bf16[128,2048]{1,0:T(8,128)(2,1)} %bitcast.22, f32[1,2048]{1,0:T(1,128)} %broadcast_in_dim.15.c, f32[128,2048]{1,0:T(8,128)} %get-tuple-element.15.trail, ...), custom_call_target="tpu_custom_call" | custom-call | tf_op jit(solution)/shard_map/final_part/pallas_call | solution.py:295
  76.7 1.5 %reshape.27 = f32[64,32,64]{2,1,0:T(8,128)S(1)} reshape(f32[64,2048]{1,0:T(8,128)} %get-tuple-element.23) | data formatting | bytes 1048576 | tf_op jit(solution)/shard_map/reshape | solution.py:303
  78.2 0.6 copy.11
  78.8 1.2 %reshape.28 = f32[1,1,32,4096]{3,2,1,0:T(8,128)} reshape(f32[32,64,64]{2,1,0:T(8,128)S(1)} %copy.11) | data formatting | bytes 1048576 | tf_op jit(solution)/shard_map/reshape | solution.py:303
Async XLA Ops:
  0.6 9.5 %collective-permute-start = (bf16[1,128,2048]{2,1,0:T(8,128)(2,1)}, bf16[1,128,2048]{2,1,0:T(8,128)(2,1)S(1)}, u32[]{:S(2)}, u32[]{:S(2)}) collective-permute-start(bf16[1,128,2048]{2,1,0:T(8,128)(2,1)} %param.9), channel_id=1, source_target_pairs={{8,0},{16,8},{24,16},{0,24},{9,1},{17,9},{25,17},{1,25},{10,2},{18... | collective-permute-start | bytes 1572872 | tf_op jit(solution)/shard_map/ppermute | solution.py:20
  10.1 0.8 copy-start

commit v2 on v1

v2 whole, which is shorter than its diff:
```python
from functools import partial

import jax
import jax.numpy as jnp
from jax import lax
from jax.experimental import pallas as pl
from jax.experimental.pallas import tpu as pltpu
from jax.sharding import PartitionSpec as P

MB = 64
LANES = 128
F32 = jnp.float32
BF16 = jnp.bfloat16
MESH = pl.DeviceIdType.MESH


def nn(a, b):
    return lax.dot_general(a, b, (((1,), (0,)), ((), ())), preferred_element_type=F32)


def nt(a, b):
    return lax.dot_general(a, b, (((1,), (1,)), ((), ())), preferred_element_type=F32)


def tn(a, b):
    return lax.dot_general(a, b, (((0,), (0,)), ((), ())), preferred_element_type=F32)


def split(x):
    high = x.astype(BF16)
    return high, (x - high.astype(F32)).astype(BF16)


def stacked(parts):
    return jnp.concatenate(parts, axis=0)


def tiles(x):
    return [x[:, i : i + LANES] for i in range(0, x.shape[1], LANES)]


def diagonal(x, dh):
    per = LANES // dh
    lane = lax.broadcasted_iota(jnp.int32, (x.shape[0], LANES), 1) // dh
    masks = [(lane == i).astype(F32).astype(BF16) for i in range(per)]
    pieces = tiles(x)
    zero = jnp.zeros((x.shape[0], LANES), x.dtype)
    rows = []
    for t, piece in enumerate(pieces):
        for i in range(per):
            row = [zero] * len(pieces)
            row[t] = piece * masks[i]
            rows.append(jnp.concatenate(row, axis=1))
    return stacked(rows)


def folded(a, b, dh):
    per = LANES // dh
    lane = lax.broadcasted_iota(jnp.int32, (dh, LANES), 1) // dh
    out = []
    for left, right in zip(tiles(a), tiles(b)):
        product = tn(left, right)
        value = product[:dh]
        for i in range(1, per):
            value = jnp.where(lane == i, product[i * dh : (i + 1) * dh], value)
        out.append(value)
    return jnp.concatenate(out, axis=1)


def rows_times(x, weights, multiply=nn):
    high, low = split(x)
    both = multiply(stacked([high, low]), weights)
    return both[: x.shape[0]] + both[x.shape[0] :]


def full_times(x, weights, multiply=nn):
    return rows_times(x, weights[0], multiply) + multiply(x.astype(BF16), weights[1])


def halves(x, dh):
    high, low = split(x)
    return diagonal(high, dh), diagonal(low, dh)


def exact_times(x, weights, multiply=nn):
    return multiply(x, weights[0]) + multiply(x, weights[1])


def doubled(a, b):
    return stacked([a, a]), stacked(split(b))


def lane_index(shape, dh):
    return lax.broadcasted_iota(jnp.int32, shape, 1) % dh


def upper_mask(width):
    row = lax.broadcasted_iota(jnp.int32, (MB, width), 0)
    return (lane_index((MB, width), MB) >= row).astype(F32)


def weight_part(k, v, c, w, dh):
    width = c.shape[1]
    row = lax.broadcasted_iota(jnp.int32, (dh, width), 0)
    eye = jnp.where(row == lane_index((dh, width), dh), 1.0, 0.0)
    weights, errors, linear = [], [], []
    for t in range(len(k)):
        e = exact_times(k[t], halves(w, dh)) - v[t].astype(F32)
        weights.append(w)
        errors.append(e)
        linear.append(eye - c * folded(k[t], k[t], dh))
        if t + 1 < len(k):
            w = w - c * folded(*doubled(k[t], e), dh)
    a = linear[-1]
    for t in range(len(k) - 2, -1, -1):
        a = full_times(linear[t], halves(a, dh))
    return weights, errors, a


def step_back(q, k, z, error_grad, dh):
    high, low = split(error_grad)
    return folded(stacked([q, k, k]), stacked([z, high, low]), dh)


def source_part(q, k, z, c, dh):
    upper = upper_mask(c.shape[1])
    carried = [
        rows_times(nt(k[t], diagonal(q[t], dh)) * upper, diagonal(z[t], dh))
        for t in range(len(k))
    ]
    b = None
    for t in range(len(k) - 1, -1, -1):
        total = carried[t] if b is None else carried[t] + exact_times(k[t], halves(b, dh))
        update = step_back(q[t], k[t], z[t], total * -c, dh)
        b = update if b is None else b + update
    return carried, b


def score_part(q, k, z, c, weights, errors, dh):
    upper = upper_mask(c.shape[1])
    query_grads, key_part = [], []
    for t in range(len(k)):
        score_grad = rows_times(errors[t], diagonal(z[t], dh), nt) * (upper * -c)
        key_part.append(rows_times(score_grad, diagonal(q[t], dh)))
        high, low = split(score_grad)
        query_grads.append(
            exact_times(z[t], halves(weights[t], dh), nt)
            + folded(stacked([high, low]), stacked([k[t], k[t]]), dh)
        )
    return query_grads, key_part


def final_part(q, k, z, c, weights, errors, carried, key_part, g, dh):
    count = len(q)
    key_grads, value_grads = [None] * count, [None] * count
    for t in range(count - 1, -1, -1):
        whole = halves(g, dh)
        minus = c * (carried[t] + exact_times(k[t], whole))
        value_grads[t] = minus
        key_grads[t] = (
            key_part[t]
            - full_times(minus, halves(weights[t], dh), nt)
            - c * full_times(errors[t], whole, nt)
        )
        high, low = split(-minus)
        g = g + folded(stacked([q[t], k[t], k[t]]), stacked([z[t], high, low]), dh)
    return key_grads, value_grads, g


def cut(ref, lanes, size=MB):
    return [ref[i : i + size, lanes] for i in range(0, ref.shape[0], size)]


def put(ref, lanes, parts):
    size = ref.shape[0] // len(parts)
    for i, part in enumerate(parts):
        ref[i * size : (i + 1) * size, lanes] = part.astype(ref.dtype)


def kernel(
    dh, width, upstream, q, k, v, c, w0,
    gq, gk, gv, start,
    z, trail, err, car, kp, a, b, other_a, other_b, pair_a, pair_b, second_a, second_b,
    entering, leaving, back, end,
    up_sems, a_send, a_recv, b_send, b_recv, g_send, g_recv, r_send, r_recv,
):
    shard, shards = lax.axis_index("seq"), lax.axis_size("seq")
    section, sections = lax.axis_index("section"), lax.axis_size("section")
    half = q.shape[1] // 2
    chunks = half // width
    side = lax.rem(shard, 2)
    partner = (section, shard + 1 - 2 * side)
    before = (section, jnp.maximum(shard - 2, 0))
    after = (section, jnp.minimum(shard + 2, shards - 1))
    below = (lax.rem(section + sections - 1, sections), shard)
    above = (lax.rem(section + 1, sections), shard)
    not_first = shard >= 2
    not_last = shard < shards - 2

    barrier = pltpu.get_barrier_semaphore()
    for peer in (below, above, partner):
        pl.semaphore_signal(barrier, inc=1, device_id=peer, device_id_type=MESH)
    for present, peer in ((not_first, before), (not_last, after)):
        @pl.when(present)
        def _():
            pl.semaphore_signal(barrier, inc=1, device_id=peer, device_id_type=MESH)
    pl.semaphore_wait(barrier, 3 + not_first.astype(jnp.int32) + not_last.astype(jnp.int32))

    def remote(source, target, send, recv, peer):
        return pltpu.make_async_remote_copy(
            src_ref=source, dst_ref=target, send_sem=send, recv_sem=recv,
            device_id=peer, device_id_type=MESH,
        )

    upward = remote(upstream, z, up_sems.at[0], up_sems.at[1], below)
    upward.start()

    def own(i):
        return pl.ds(pl.multiple_of(side * half + i * width, width), width)

    def others(i):
        return pl.ds(pl.multiple_of((1 - side) * half + i * width, width), width)

    def place(i):
        return pl.ds(pl.multiple_of(i * width, width), width)

    def send_a(i):
        return remote(a.at[:, others(i)], other_a.at[:, place(i)], a_send.at[i], a_recv.at[i], partner)

    def send_b(i):
        return remote(b.at[:, others(i)], other_b.at[:, place(i)], b_send.at[i], b_recv.at[i], partner)

    def send_g(i):
        return remote(leaving.at[:, place(i)], entering.at[:, place(i)], g_send.at[i], g_recv.at[i], before)

    def send_r(i):
        return remote(back.at[:, place(i)], end.at[:, own(i)], r_send.at[i], r_recv.at[i], partner)

    def await_r(i):
        return remote(back.at[:, place(i)], end.at[:, others(i)], r_send.at[i], r_recv.at[i], partner)

    def weights_of(lanes):
        weights, errors, linear = weight_part(
            cut(k, lanes), cut(v, lanes), c[:, lanes], w0[:, lanes], dh
        )
        put(trail, lanes, weights)
        put(err, lanes, errors)
        a[:, lanes] = linear

    def sources_of(lanes):
        carried, offset = source_part(cut(q, lanes), cut(k, lanes), cut(z, lanes), c[:, lanes], dh)
        put(car, lanes, carried)
        b[:, lanes] = offset

    def scores_of(lanes):
        query_grads, key_part = score_part(
            cut(q, lanes), cut(k, lanes), cut(z, lanes), c[:, lanes],
            cut(trail, lanes, dh), cut(err, lanes), dh,
        )
        put(gq, lanes, query_grads)
        put(kp, lanes, key_part)

    def finals_of(lanes):
        key_grads, value_grads, first = final_part(
            cut(q, lanes), cut(k, lanes), cut(z, lanes), c[:, lanes],
            cut(trail, lanes, dh), cut(err, lanes), cut(car, lanes), cut(kp, lanes), end[:, lanes], dh,
        )
        put(gk, lanes, key_grads)
        put(gv, lanes, value_grads)
        start[:, lanes] = first

    def each(body):
        def step(i, nothing):
            body(i)
            return nothing

        lax.fori_loop(0, chunks, step, jnp.int32(0))

    def first_step(i):
        weights_of(others(i))
        weights_of(own(i))
        send_a(i).start()

    def second_step(i):
        sources_of(others(i))
        send_b(i).start()
        sources_of(own(i))

    is_even = side == 0

    def pair_step(i):
        lanes, local = own(i), place(i)
        send_a(i).wait_recv()
        send_b(i).wait_recv()
        near_a, near_b = a[:, lanes], b[:, lanes]
        far_a, far_b = other_a[:, local], other_b[:, local]
        a1 = jnp.where(is_even, far_a, near_a)
        b1 = jnp.where(is_even, far_b, near_b)
        a0 = jnp.where(is_even, near_a, far_a)
        b0 = jnp.where(is_even, near_b, far_b)
        offset = full_times(a0, halves(b1, dh)) + b0
        leaving[:, local] = offset

        @pl.when(not_first & jnp.logical_not(not_last))
        def _():
            send_g(i).start()

        pair_b[:, local] = offset
        pair_a[:, local] = full_times(a0, halves(a1, dh))
        second_a[:, local] = a1
        second_b[:, local] = b1

    def relay_step(i):
        lanes, local = own(i), place(i)
        scores_of(others(i))
        scores_of(lanes)

        @pl.when(not_last)
        def _():
            send_g(i).wait_recv()
            incoming = entering[:, local]
            whole = halves(incoming, dh)
            leaving[:, local] = full_times(pair_a[:, local], whole) + pair_b[:, local]

            @pl.when(not_first)
            def _():
                send_g(i).start()

            middle = full_times(second_a[:, local], whole) + second_b[:, local]
            back[:, local] = jnp.where(is_even, incoming, middle)
            end[:, lanes] = jnp.where(is_even, middle, incoming)

        @pl.when(jnp.logical_not(not_last))
        def _():
            middle = second_b[:, local]
            nothing = jnp.zeros_like(middle)
            back[:, local] = jnp.where(is_even, nothing, middle)
            end[:, lanes] = jnp.where(is_even, middle, nothing)

        send_r(i).start()

    def last_step(i):
        finals_of(own(i))
        await_r(i).wait_recv()
        finals_of(others(i))

    def drain(i):
        send_a(i).wait_send()
        send_b(i).wait_send()
        send_r(i).wait_send()

        @pl.when(not_first)
        def _():
            send_g(i).wait_send()

    each(first_step)
    upward.wait_recv()
    each(second_step)
    each(pair_step)
    each(relay_step)
    each(last_step)
    each(drain)
    upward.wait_send()


def per_device(queries, memory_keys, memory_values, upstream, inner_rate, checkpoints):
    heads = inner_rate.shape[1]
    features = queries.shape[2]
    dh = features // heads
    tokens = queries.shape[1]
    width = 2 * LANES
    half = features // 2
    chunks = half // width
    count = tokens // MB

    c = jnp.repeat(inner_rate / MB, dh, axis=1)
    initial = checkpoints.reshape(heads, dh, dh).transpose(1, 0, 2).reshape(dh, features)
    vmem = pl.BlockSpec(memory_space=pltpu.VMEM)
    tall = jax.ShapeDtypeStruct((tokens, features), BF16)
    whole = pltpu.VMEM((dh, features), F32)
    part = pltpu.VMEM((dh, half), F32)
    rows = pltpu.VMEM((tokens, features), F32)
    gq, gk, gv, start = pl.pallas_call(
        partial(kernel, dh, width),
        in_specs=[pl.BlockSpec(memory_space=pl.ANY)] + [vmem] * 5,
        out_specs=[vmem] * 4,
        out_shape=[tall, tall, tall, jax.ShapeDtypeStruct((dh, features), F32)],
        scratch_shapes=[
            pltpu.VMEM((tokens, features), BF16),
            pltpu.VMEM((count * dh, features), F32),
            rows, rows, rows,
            whole, whole,
            part, part, part, part, part, part, part, part, part,
            whole,
            pltpu.SemaphoreType.DMA((2,)),
        ] + [pltpu.SemaphoreType.DMA((chunks,))] * 8,
        compiler_params=pltpu.CompilerParams(collective_id=0, has_side_effects=True),
        name="layer_backward",
    )(upstream[0], queries[0], memory_keys[0], memory_values[0], c, initial)
    start = start.reshape(dh, heads, dh).transpose(1, 0, 2).reshape(1, 1, heads, dh * dh)
    return gq[None], gk[None], gv[None], start


def solution(mesh):
    return jax.shard_map(
        per_device,
        mesh=mesh,
        in_specs=(
            P("section", "seq", None),
            P("section", "seq", None),
            P("section", "seq", None),
            P("section", "seq", None),
            P("section", None),
            P("section", "seq", None, None),
        ),
        out_specs=(
            P("section", "seq", None),
            P("section", "seq", None),
            P("section", "seq", None),
            P("section", "seq", None, None),
        ),
        check_vma=False,
    )
```

time: 80.4 us -> 59.4 us (0.74)
  the two profiles are of different devices: /device:TPU:0 before, /device:TPU:1 now
where the time goes in v2:
time: 59.4 us; the launch traced here: 59 us
  Pallas kernels  47.2 us (79%)
  local copies, waits for them, and re-layouts  11.1 us (19%)
  between operations  0.69 us (1%)
    pallas_call x1, Pallas kernels, per_device(): pl.pallas_call(partial(kernel, dh, width), in_specs=[pl.BlockSpec(memory_...  47.2 us
    unnamed x11, local copies, waits for them, and re-layouts  3.9 us
    reshape x3, local copies, waits for them, and re-layouts, per_device(): checkpoints.reshape(heads, dh, dh).transpose(1, 0, 2).reshape(dh, features)  3.22 us
    reshape x2, local copies, waits for them, and re-layouts, per_device(): start.reshape(dh, heads, dh).transpose(1, 0, 2)  2.61 us

profile of v2, /device:TPU:1, one launch (start us, length us, event | category | flops | bytes accessed | tf_op | source)
XLA Modules:
  0.0 59.0 jit_solution(11413897672563831632)
XLA Ops:
  0.6 0.0 copy-start.3
  0.6 0.6 %copy-done.3 = f32[1,32]{1,0:T(1,128)S(1)} copy-done((f32[1,32]{1,0:T(1,128)S(1)}, f32[1,32]{1,0:T(1,128)}, u32[]{:S(2)}) %copy-start.3) | copy-done | bytes 152
  1.3 0.1 broadcast_in_dim.14
  1.4 0.7 %broadcast_in_dim.15.c = f32[1,2048]{1,0:T(1,128)} reshape(f32[32,64]{1,0:T(8,128)S(1)} %broadcast_in_dim.14) | data formatting | bytes 16384 | tf_op jit(solution)/shard_map/broadcast_in_dim | solution.py:376
  2.0 1.5 %reshape.25 = f32[32,64,64]{2,1,0:T(8,128)S(1)} reshape(f32[1,1,32,4096]{3,2,1,0:T(8,128)} %param.11) | data formatting | bytes 1048576 | tf_op jit(solution)/shard_map/reshape | solution.py:377
  3.5 0.6 %copy.13 = f32[32,64,64]{2,0,1:T(8,128)S(1)} copy(f32[32,64,64]{2,1,0:T(8,128)S(1)} %reshape.25) | data formatting | bytes 1048576 | tf_op jit(solution)/shard_map/reshape | solution.py:377
  4.1 1.2 %reshape.26.w0 = f32[64,2048]{1,0:T(8,128)} reshape(f32[64,32,64]{2,1,0:T(8,128)S(1)} %bitcast.15) | data formatting | bytes 1048576 | tf_op jit(solution)/shard_map/reshape | solution.py:377
  5.3 47.2 %layer_backward.1 = (bf16[128,2048]{1,0:T(8,128)(2,1)}, bf16[128,2048]{1,0:T(8,128)(2,1)}, bf16[128,2048]{1,0:T(8,128)(2,1)}, f32[64,2048]{1,0:T(8,128)}) custom-call(bf16[128,2048]{1,0:T(8,128)(2,1)} %bitcast.17, bf16[128,2048]{1,0:T(8,128)(2,1)} %bitcast.18, bf16[128,2048]{1,0:T(8,128)(2,1)} %bitcast.19, bf16[128,2048]{1,0:T(8,128)(2,1)} %bitcast.20, ...), custom_call_target="tpu_custom_call" | custom-call | tf_op jit(solution)/shard_map/layer_backward/pallas_call | solution.py:383
  52.5 1.5 %reshape.27 = f32[64,32,64]{2,1,0:T(8,128)S(1)} reshape(f32[64,2048]{1,0:T(8,128)} %get-tuple-element.11) | data formatting | bytes 1048576 | tf_op jit(solution)/shard_map/reshape | solution.py:400
  54.0 0.6 %copy.11 = f32[32,64,64]{2,1,0:T(8,128)S(1)} copy(f32[32,64,64]{2,0,1:T(8,128)S(1)} %bitcast.16) | data formatting | bytes 1048576 | tf_op jit(solution)/shard_map/transpose | solution.py:400
  54.6 0.0 copy-start.2
  54.6 1.2 %reshape.28 = f32[1,1,32,4096]{3,2,1,0:T(8,128)} reshape(f32[32,64,64]{2,1,0:T(8,128)S(1)} %copy.11) | data formatting | bytes 1048576 | tf_op jit(solution)/shard_map/reshape | solution.py:400
  55.8 0.0 copy-done.2
  55.8 0.0 copy-start.1
  55.8 0.8 %copy.17 = bf16[1,128,2048]{2,1,0:T(8,128)(2,1)} copy(bf16[1,128,2048]{2,1,0:T(8,128)(2,1)S(1)} %bitcast.23) | data formatting | bytes 1048576
  56.6 0.4 copy-done.1
  57.0 0.0 copy-start
  57.0 0.8 %copy.18 = bf16[1,128,2048]{2,1,0:T(8,128)(2,1)} copy(bf16[1,128,2048]{2,1,0:T(8,128)(2,1)S(1)} %bitcast.22) | data formatting | bytes 1048576
  57.8 0.4 copy-done
  58.2 0.8 %copy.19 = bf16[1,128,2048]{2,1,0:T(8,128)(2,1)} copy(bf16[1,128,2048]{2,1,0:T(8,128)(2,1)S(1)} %bitcast.21) | data formatting | bytes 1048576
  (1 shorter events, 0.0 us)
Async XLA Ops:
  0.6 0.7 %copy-start.3 = (f32[1,32]{1,0:T(1,128)S(1)}, f32[1,32]{1,0:T(1,128)}, u32[]{:S(2)}) copy-start(f32[1,32]{1,0:T(1,128)} %param.10) | copy-start | bytes 388
  54.6 1.2 %copy-start.2 = (bf16[128,2048]{1,0:T(8,128)(2,1)S(1)}, bf16[128,2048]{1,0:T(8,128)(2,1)}, u32[]{:S(2)}) copy-start(bf16[128,2048]{1,0:T(8,128)(2,1)} %get-tuple-element.8) | copy-start | bytes 1572868
  55.8 1.2 %copy-start.1 = (bf16[128,2048]{1,0:T(8,128)(2,1)S(1)}, bf16[128,2048]{1,0:T(8,128)(2,1)}, u32[]{:S(2)}) copy-start(bf16[128,2048]{1,0:T(8,128)(2,1)} %get-tuple-element.9) | copy-start | bytes 1572868
  57.0 1.2 %copy-start = (bf16[128,2048]{1,0:T(8,128)(2,1)S(1)}, bf16[128,2048]{1,0:T(8,128)(2,1)}, u32[]{:S(2)}) copy-start(bf16[128,2048]{1,0:T(8,128)(2,1)} %get-tuple-element.10) | copy-start | bytes 1572868

commit v3 on v2

--- a/solution.py
+++ b/solution.py
@@ -106,17 +106,32 @@
     weights, errors, linear = [], [], []
     for t in range(len(k)):
         e = exact_times(k[t], halves(w, dh)) - v[t].astype(F32)
+        yield
         weights.append(w)
         errors.append(e)
-        linear.append(eye - c * folded(k[t], k[t], dh))
         if t + 1 < len(k):
             w = w - c * folded(*doubled(k[t], e), dh)
+            yield
+        linear.append(eye - c * folded(k[t], k[t], dh))
+        yield
     a = linear[-1]
     for t in range(len(k) - 2, -1, -1):
         a = full_times(linear[t], halves(a, dh))
     return weights, errors, a
 
 
+def interleaved(runs):
+    results, waiting = [None] * len(runs), dict(enumerate(runs))
+    while waiting:
+        for i, run in list(waiting.items()):
+            try:
+                next(run)
+            except StopIteration as stop:
+                results[i] = stop.value
+                del waiting[i]
+    return results
+
+
 def step_back(q, k, z, error_grad, dh):
     high, low = split(error_grad)
     return folded(stacked([q, k, k]), stacked([z, high, low]), dh)
@@ -124,15 +139,19 @@
 
 def source_part(q, k, z, c, dh):
     upper = upper_mask(c.shape[1])
-    carried = [
-        rows_times(nt(k[t], diagonal(q[t], dh)) * upper, diagonal(z[t], dh))
-        for t in range(len(k))
-    ]
+    carried = [None] * len(k)
+    for t in range(len(k) - 1, -1, -1):
+        scores = nt(k[t], diagonal(q[t], dh)) * upper
+        yield
+        carried[t] = rows_times(scores, diagonal(z[t], dh))
+        yield
     b = None
     for t in range(len(k) - 1, -1, -1):
         total = carried[t] if b is None else carried[t] + exact_times(k[t], halves(b, dh))
+        yield
         update = step_back(q[t], k[t], z[t], total * -c, dh)
         b = update if b is None else b + update
+        yield
     return carried, b
 
 
@@ -141,12 +160,15 @@
     query_grads, key_part = [], []
     for t in range(len(k)):
         score_grad = rows_times(errors[t], diagonal(z[t], dh), nt) * (upper * -c)
+        yield
         key_part.append(rows_times(score_grad, diagonal(q[t], dh)))
+        yield
         high, low = split(score_grad)
         query_grads.append(
             exact_times(z[t], halves(weights[t], dh), nt)
             + folded(stacked([high, low]), stacked([k[t], k[t]]), dh)
         )
+        yield
     return query_grads, key_part
 
 
@@ -156,14 +178,14 @@
     for t in range(count - 1, -1, -1):
         whole = halves(g, dh)
         minus = c * (carried[t] + exact_times(k[t], whole))
+        yield
         value_grads[t] = minus
-        key_grads[t] = (
-            key_part[t]
-            - full_times(minus, halves(weights[t], dh), nt)
-            - c * full_times(errors[t], whole, nt)
-        )
-        high, low = split(-minus)
-        g = g + folded(stacked([q[t], k[t], k[t]]), stacked([z[t], high, low]), dh)
+        g = g + step_back(q[t], k[t], z[t], -minus, dh)
+        yield
+        partial_grad = key_part[t] - c * full_times(errors[t], whole, nt)
+        yield
+        key_grads[t] = partial_grad - full_times(minus, halves(weights[t], dh), nt)
+        yield
     return key_grads, value_grads, g
 
 
@@ -239,32 +261,50 @@
     def await_r(i):
         return remote(back.at[:, place(i)], end.at[:, others(i)], r_send.at[i], r_recv.at[i], partner)
 
+    def narrow(span):
+        start_lane = span.start
+        return [
+            pl.ds(pl.multiple_of(start_lane + j, LANES), LANES) for j in range(0, width, LANES)
+        ]
+
+    def together(compute, store, spans):
+        groups = [lanes for span in spans for lanes in narrow(span)]
+        results = interleaved([compute(lanes) for lanes in groups])
+        for lanes, result in zip(groups, results):
+            store(lanes, *result)
+
     def weights_of(lanes):
-        weights, errors, linear = weight_part(
-            cut(k, lanes), cut(v, lanes), c[:, lanes], w0[:, lanes], dh
-        )
+        return weight_part(cut(k, lanes), cut(v, lanes), c[:, lanes], w0[:, lanes], dh)
+
+    def put_weights(lanes, weights, errors, linear):
         put(trail, lanes, weights)
         put(err, lanes, errors)
         a[:, lanes] = linear
 
     def sources_of(lanes):
-        carried, offset = source_part(cut(q, lanes), cut(k, lanes), cut(z, lanes), c[:, lanes], dh)
+        return source_part(cut(q, lanes), cut(k, lanes), cut(z, lanes), c[:, lanes], dh)
+
+    def put_sources(lanes, carried, offset):
         put(car, lanes, carried)
         b[:, lanes] = offset
 
     def scores_of(lanes):
-        query_grads, key_part = score_part(
+        return score_part(
             cut(q, lanes), cut(k, lanes), cut(z, lanes), c[:, lanes],
             cut(trail, lanes, dh), cut(err, lanes), dh,
         )
+
+    def put_scores(lanes, query_grads, key_part):
         put(gq, lanes, query_grads)
         put(kp, lanes, key_part)
 
     def finals_of(lanes):
-        key_grads, value_grads, first = final_part(
+        return final_part(
             cut(q, lanes), cut(k, lanes), cut(z, lanes), c[:, lanes],
             cut(trail, lanes, dh), cut(err, lanes), cut(car, lanes), cut(kp, lanes), end[:, lanes], dh,
         )
+
+    def put_finals(lanes, key_grads, value_grads, first):
         put(gk, lanes, key_grads)
         put(gv, lanes, value_grads)
         start[:, lanes] = first
@@ -277,14 +317,12 @@
         lax.fori_loop(0, chunks, step, jnp.int32(0))
 
     def first_step(i):
-        weights_of(others(i))
-        weights_of(own(i))
+        together(weights_of, put_weights, [others(i), own(i)])
         send_a(i).start()
 
     def second_step(i):
-        sources_of(others(i))
+        together(sources_of, put_sources, [others(i), own(i)])
         send_b(i).start()
-        sources_of(own(i))
 
     is_even = side == 0
 
@@ -312,8 +350,7 @@
 
     def relay_step(i):
         lanes, local = own(i), place(i)
-        scores_of(others(i))
-        scores_of(lanes)
+        together(scores_of, put_scores, [others(i), lanes])
 
         @pl.when(not_last)
         def _():
@@ -340,9 +377,8 @@
         send_r(i).start()
 
     def last_step(i):
-        finals_of(own(i))
         await_r(i).wait_recv()
-        finals_of(others(i))
+        together(finals_of, put_finals, [own(i), others(i)])
 
     def drain(i):
         send_a(i).wait_send()

time: 59.4 us -> 52.7 us (0.89)
  Pallas kernels: 47.2 us -> 40.6 us
    pallas_call x1, Pallas kernels: 47.2 us -> 40.6 us  [per_device(): pl.pallas_call(partial(kernel, dh, width), in_specs=[pl.BlockSpec(memory_...]
where the time goes in v3:
time: 52.7 us; the launch traced here: 52.4 us
  Pallas kernels  40.6 us (77%)
  local copies, waits for them, and re-layouts  11.1 us (21%)
  between operations  0.69 us (1%)
    pallas_call x1, Pallas kernels, per_device(): pl.pallas_call(partial(kernel, dh, width), in_specs=[pl.BlockSpec(memory_...  40.6 us
    unnamed x11, local copies, waits for them, and re-layouts  3.9 us
    reshape x3, local copies, waits for them, and re-layouts, per_device(): checkpoints.reshape(heads, dh, dh).transpose(1, 0, 2).reshape(dh, features)  3.22 us
    reshape x2, local copies, waits for them, and re-layouts, per_device(): start.reshape(dh, heads, dh).transpose(1, 0, 2)  2.61 us

profile of v3, /device:TPU:1, one launch (start us, length us, event | category | flops | bytes accessed | tf_op | source)
XLA Modules:
  0.0 52.4 jit_solution(6739614235921966325)
XLA Ops:
  0.6 0.0 copy-start.3
  0.6 0.6 %copy-done.3 = f32[1,32]{1,0:T(1,128)S(1)} copy-done((f32[1,32]{1,0:T(1,128)S(1)}, f32[1,32]{1,0:T(1,128)}, u32[]{:S(2)}) %copy-start.3) | copy-done | bytes 152
  1.3 0.1 broadcast_in_dim.14
  1.4 0.7 %broadcast_in_dim.15.c = f32[1,2048]{1,0:T(1,128)} reshape(f32[32,64]{1,0:T(8,128)S(1)} %broadcast_in_dim.14) | data formatting | bytes 16384 | tf_op jit(solution)/shard_map/broadcast_in_dim | solution.py:412
  2.0 1.5 %reshape.25 = f32[32,64,64]{2,1,0:T(8,128)S(1)} reshape(f32[1,1,32,4096]{3,2,1,0:T(8,128)} %param.11) | data formatting | bytes 1048576 | tf_op jit(solution)/shard_map/reshape | solution.py:413
  3.5 0.6 %copy.13 = f32[32,64,64]{2,0,1:T(8,128)S(1)} copy(f32[32,64,64]{2,1,0:T(8,128)S(1)} %reshape.25) | data formatting | bytes 1048576 | tf_op jit(solution)/shard_map/reshape | solution.py:413
  4.1 1.2 %reshape.26.w0 = f32[64,2048]{1,0:T(8,128)} reshape(f32[64,32,64]{2,1,0:T(8,128)S(1)} %bitcast.15) | data formatting | bytes 1048576 | tf_op jit(solution)/shard_map/reshape | solution.py:413
  5.3 40.6 %layer_backward.1 = (bf16[128,2048]{1,0:T(8,128)(2,1)}, bf16[128,2048]{1,0:T(8,128)(2,1)}, bf16[128,2048]{1,0:T(8,128)(2,1)}, f32[64,2048]{1,0:T(8,128)}) custom-call(bf16[128,2048]{1,0:T(8,128)(2,1)} %bitcast.17, bf16[128,2048]{1,0:T(8,128)(2,1)} %bitcast.18, bf16[128,2048]{1,0:T(8,128)(2,1)} %bitcast.19, bf16[128,2048]{1,0:T(8,128)(2,1)} %bitcast.20, ...), custom_call_target="tpu_custom_call" | custom-call | tf_op jit(solution)/shard_map/layer_backward/pallas_call | solution.py:419
  45.9 1.5 %reshape.27 = f32[64,32,64]{2,1,0:T(8,128)S(1)} reshape(f32[64,2048]{1,0:T(8,128)} %get-tuple-element.11) | data formatting | bytes 1048576 | tf_op jit(solution)/shard_map/reshape | solution.py:436
  47.3 0.6 %copy.11 = f32[32,64,64]{2,1,0:T(8,128)S(1)} copy(f32[32,64,64]{2,0,1:T(8,128)S(1)} %bitcast.16) | data formatting | bytes 1048576 | tf_op jit(solution)/shard_map/transpose | solution.py:436
  47.9 0.0 copy-start.2
  47.9 1.2 %reshape.28 = f32[1,1,32,4096]{3,2,1,0:T(8,128)} reshape(f32[32,64,64]{2,1,0:T(8,128)S(1)} %copy.11) | data formatting | bytes 1048576 | tf_op jit(solution)/shard_map/reshape | solution.py:436
  49.1 0.0 copy-done.2
  49.1 0.0 copy-start.1
  49.1 0.8 %copy.17 = bf16[1,128,2048]{2,1,0:T(8,128)(2,1)} copy(bf16[1,128,2048]{2,1,0:T(8,128)(2,1)S(1)} %bitcast.23) | data formatting | bytes 1048576
  49.9 0.4 copy-done.1
  50.3 0.0 copy-start
  50.3 0.8 %copy.18 = bf16[1,128,2048]{2,1,0:T(8,128)(2,1)} copy(bf16[1,128,2048]{2,1,0:T(8,128)(2,1)S(1)} %bitcast.22) | data formatting | bytes 1048576
  51.1 0.4 copy-done
  51.6 0.8 %copy.19 = bf16[1,128,2048]{2,1,0:T(8,128)(2,1)} copy(bf16[1,128,2048]{2,1,0:T(8,128)(2,1)S(1)} %bitcast.21) | data formatting | bytes 1048576
  (1 shorter events, 0.0 us)
Async XLA Ops:
  0.6 0.7 %copy-start.3 = (f32[1,32]{1,0:T(1,128)S(1)}, f32[1,32]{1,0:T(1,128)}, u32[]{:S(2)}) copy-start(f32[1,32]{1,0:T(1,128)} %param.10) | copy-start | bytes 388
  47.9 1.2 %copy-start.2 = (bf16[128,2048]{1,0:T(8,128)(2,1)S(1)}, bf16[128,2048]{1,0:T(8,128)(2,1)}, u32[]{:S(2)}) copy-start(bf16[128,2048]{1,0:T(8,128)(2,1)} %get-tuple-element.8) | copy-start | bytes 1572868
  49.1 1.2 %copy-start.1 = (bf16[128,2048]{1,0:T(8,128)(2,1)S(1)}, bf16[128,2048]{1,0:T(8,128)(2,1)}, u32[]{:S(2)}) copy-start(bf16[128,2048]{1,0:T(8,128)(2,1)} %get-tuple-element.9) | copy-start | bytes 1572868
  50.3 1.2 %copy-start = (bf16[128,2048]{1,0:T(8,128)(2,1)S(1)}, bf16[128,2048]{1,0:T(8,128)(2,1)}, u32[]{:S(2)}) copy-start(bf16[128,2048]{1,0:T(8,128)(2,1)} %get-tuple-element.10) | copy-start | bytes 1572868

commit v4 on v3

--- a/solution.py
+++ b/solution.py
@@ -200,15 +200,17 @@
 
 
 def kernel(
-    dh, width, upstream, q, k, v, c, w0,
+    dh, width, upstream, q, k, v, rates, checkpoint,
     gq, gk, gv, start,
+    rows_of_heads, stage,
     z, trail, err, car, kp, a, b, other_a, other_b, pair_a, pair_b, second_a, second_b,
     entering, leaving, back, end,
-    up_sems, a_send, a_recv, b_send, b_recv, g_send, g_recv, r_send, r_recv,
+    line_sem, up_sems, a_send, a_recv, b_send, b_recv, g_send, g_recv, r_send, r_recv,
 ):
     shard, shards = lax.axis_index("seq"), lax.axis_size("seq")
     section, sections = lax.axis_index("section"), lax.axis_size("section")
-    half = q.shape[1] // 2
+    features = q.shape[1]
+    half = features // 2
     chunks = half // width
     side = lax.rem(shard, 2)
     partner = (section, shard + 1 - 2 * side)
@@ -237,6 +239,59 @@
     upward = remote(upstream, z, up_sems.at[0], up_sems.at[1], below)
     upward.start()
 
+    heads = features // dh
+    lines = dh * dh // LANES
+
+    def line_in(i):
+        return pltpu.make_async_copy(
+            checkpoint.at[:, pl.ds(i * LANES, LANES)],
+            rows_of_heads.at[pl.ds(i * heads, heads), :],
+            line_sem.at[i],
+        )
+
+    def line_out(i):
+        return pltpu.make_async_copy(
+            rows_of_heads.at[pl.ds(i * heads, heads), :],
+            start.at[:, pl.ds(i * LANES, LANES)],
+            line_sem.at[i],
+        )
+
+    for i in range(lines):
+        line_in(i).start()
+    for i in range(lines):
+        line_in(i).wait()
+
+    left = lax.broadcasted_iota(jnp.int32, (lines, LANES), 1) < dh
+
+    def swap(x):
+        return jnp.concatenate([x[:, dh:], x[:, :dh]], axis=1)
+
+    def head_of(lanes):
+        return (lanes.start // LANES) * (LANES // dh)
+
+    def rate_of(lanes):
+        head = head_of(lanes)
+        first = lax.broadcasted_iota(jnp.int32, (1, LANES), 1) < dh
+        return jnp.where(first, rates[0, head], rates[0, head + 1]) / MB
+
+    def load_weight(lanes):
+        head = head_of(lanes)
+        x = rows_of_heads[pl.ds(head, lines, stride=heads), :]
+        y = rows_of_heads[pl.ds(head + 1, lines, stride=heads), :]
+        base = head * (dh // 2)
+        stage[pl.ds(base, lines, stride=2), :] = jnp.where(left, x, swap(y))
+        stage[pl.ds(base + 1, lines, stride=2), :] = jnp.where(left, swap(x), y)
+        trail[:dh, lanes] = stage[pl.ds(pl.multiple_of(base, dh), dh), :]
+
+    def store_start(lanes, first):
+        head = head_of(lanes)
+        base = head * (dh // 2)
+        stage[pl.ds(pl.multiple_of(base, dh), dh), :] = first
+        even = stage[pl.ds(base, lines, stride=2), :]
+        odd = stage[pl.ds(base + 1, lines, stride=2), :]
+        rows_of_heads[pl.ds(head, lines, stride=heads), :] = jnp.where(left, even, swap(odd))
+        rows_of_heads[pl.ds(head + 1, lines, stride=heads), :] = jnp.where(left, swap(even), odd)
+
     def own(i):
         return pl.ds(pl.multiple_of(side * half + i * width, width), width)
 
@@ -274,15 +329,16 @@
             store(lanes, *result)
 
     def weights_of(lanes):
-        return weight_part(cut(k, lanes), cut(v, lanes), c[:, lanes], w0[:, lanes], dh)
+        return weight_part(cut(k, lanes), cut(v, lanes), rate_of(lanes), trail[:dh, lanes], dh)
 
     def put_weights(lanes, weights, errors, linear):
-        put(trail, lanes, weights)
+        for t in range(1, len(weights)):
+            trail[t * dh : (t + 1) * dh, lanes] = weights[t]
         put(err, lanes, errors)
         a[:, lanes] = linear
 
     def sources_of(lanes):
-        return source_part(cut(q, lanes), cut(k, lanes), cut(z, lanes), c[:, lanes], dh)
+        return source_part(cut(q, lanes), cut(k, lanes), cut(z, lanes), rate_of(lanes), dh)
 
     def put_sources(lanes, carried, offset):
         put(car, lanes, carried)
@@ -290,7 +346,7 @@
 
     def scores_of(lanes):
         return score_part(
-            cut(q, lanes), cut(k, lanes), cut(z, lanes), c[:, lanes],
+            cut(q, lanes), cut(k, lanes), cut(z, lanes), rate_of(lanes),
             cut(trail, lanes, dh), cut(err, lanes), dh,
         )
 
@@ -300,14 +356,14 @@
 
     def finals_of(lanes):
         return final_part(
-            cut(q, lanes), cut(k, lanes), cut(z, lanes), c[:, lanes],
+            cut(q, lanes), cut(k, lanes), cut(z, lanes), rate_of(lanes),
             cut(trail, lanes, dh), cut(err, lanes), cut(car, lanes), cut(kp, lanes), end[:, lanes], dh,
         )
 
     def put_finals(lanes, key_grads, value_grads, first):
         put(gk, lanes, key_grads)
         put(gv, lanes, value_grads)
-        start[:, lanes] = first
+        store_start(lanes, first)
 
     def each(body):
         def step(i, nothing):
@@ -317,6 +373,9 @@
         lax.fori_loop(0, chunks, step, jnp.int32(0))
 
     def first_step(i):
+        for span in (others(i), own(i)):
+            for lanes in narrow(span):
+                load_weight(lanes)
         together(weights_of, put_weights, [others(i), own(i)])
         send_a(i).start()
 
@@ -395,8 +454,12 @@
     each(pair_step)
     each(relay_step)
     each(last_step)
+    for i in range(lines):
+        line_out(i).start()
     each(drain)
     upward.wait_send()
+    for i in range(lines):
+        line_out(i).wait()
 
 
 def per_device(queries, memory_keys, memory_values, upstream, inner_rate, checkpoints):
@@ -409,32 +472,35 @@
     chunks = half // width
     count = tokens // MB
 
-    c = jnp.repeat(inner_rate / MB, dh, axis=1)
-    initial = checkpoints.reshape(heads, dh, dh).transpose(1, 0, 2).reshape(dh, features)
     vmem = pl.BlockSpec(memory_space=pltpu.VMEM)
+    hbm = pl.BlockSpec(memory_space=pl.ANY)
+    assert 2 * dh == LANES
+    lines = dh * dh // LANES
     tall = jax.ShapeDtypeStruct((tokens, features), BF16)
     whole = pltpu.VMEM((dh, features), F32)
     part = pltpu.VMEM((dh, half), F32)
     rows = pltpu.VMEM((tokens, features), F32)
     gq, gk, gv, start = pl.pallas_call(
         partial(kernel, dh, width),
-        in_specs=[pl.BlockSpec(memory_space=pl.ANY)] + [vmem] * 5,
-        out_specs=[vmem] * 4,
-        out_shape=[tall, tall, tall, jax.ShapeDtypeStruct((dh, features), F32)],
+        in_specs=[hbm] + [vmem] * 3 + [pl.BlockSpec(memory_space=pltpu.SMEM), hbm],
+        out_specs=[vmem] * 3 + [hbm],
+        out_shape=[tall, tall, tall, jax.ShapeDtypeStruct((heads, dh * dh), F32)],
         scratch_shapes=[
+            pltpu.VMEM((lines * heads, LANES), F32),
+            pltpu.VMEM((features // LANES * dh, LANES), F32),
             pltpu.VMEM((tokens, features), BF16),
             pltpu.VMEM((count * dh, features), F32),
             rows, rows, rows,
             whole, whole,
             part, part, part, part, part, part, part, part, part,
             whole,
+            pltpu.SemaphoreType.DMA((lines,)),
             pltpu.SemaphoreType.DMA((2,)),
         ] + [pltpu.SemaphoreType.DMA((chunks,))] * 8,
         compiler_params=pltpu.CompilerParams(collective_id=0, has_side_effects=True),
         name="layer_backward",
-    )(upstream[0], queries[0], memory_keys[0], memory_values[0], c, initial)
-    start = start.reshape(dh, heads, dh).transpose(1, 0, 2).reshape(1, 1, heads, dh * dh)
-    return gq[None], gk[None], gv[None], start
+    )(upstream[0], queries[0], memory_keys[0], memory_values[0], inner_rate, checkpoints[0, 0])
+    return gq[None], gk[None], gv[None], start[None, None]
 
 
 def solution(mesh):

time: 52.7 us -> 47.2 us (0.90)
  local copies, waits for them, and re-layouts: 11.1 us -> 5.19 us
    reshape x5 -> x0, local copies, waits for them, and re-layouts: 5.82 us -> none  [the longest x3 3.22 us: per_device(): checkpoints.reshape(heads, dh, dh).transpose(1, 0, 2).reshape(dh, features)]
    unnamed x11 -> x10, local copies, waits for them, and re-layouts: 3.9 us -> 5.19 us
    broadcast_in_dim x2 -> x0, local copies, waits for them, and re-layouts: 0.75 us -> none  [per_device(): c = jnp.repeat(inner_rate / MB, dh, axis=1)]
    transpose x1 -> x0, local copies, waits for them, and re-layouts: 0.61 us -> none  [per_device(): start.reshape(dh, heads, dh).transpose(1, 0, 2)]
where the time goes in v4:
time: 47.2 us; the launch traced here: 46.9 us
  Pallas kernels  41 us (87%)
  local copies, waits for them, and re-layouts  5.19 us (11%)
  between operations  0.65 us (1%)
    pallas_call x1, Pallas kernels, per_device(): pl.pallas_call(partial(kernel, dh, width), in_specs=[hbm] + [vmem] * 3 +...  41 us
    unnamed x10, local copies, waits for them, and re-layouts  5.19 us

profile of v4, /device:TPU:1, one launch (start us, length us, event | category | flops | bytes accessed | tf_op | source)
XLA Modules:
  0.0 46.9 jit_solution(1500088012008441927)
XLA Ops:
  0.6 41.0 %layer_backward.1 = (bf16[128,2048]{1,0:T(8,128)(2,1)}, bf16[128,2048]{1,0:T(8,128)(2,1)}, bf16[128,2048]{1,0:T(8,128)(2,1)}, f32[32,4096]{1,0:T(8,128)}) custom-call(bf16[128,2048]{1,0:T(8,128)(2,1)} %bitcast.13, bf16[128,2048]{1,0:T(8,128)(2,1)} %bitcast.14, bf16[128,2048]{1,0:T(8,128)(2,1)} %bitcast.15, bf16[128,2048]{1,0:T(8,128)(2,1)} %bitcast.16, ...), custom_call_target="tpu_custom_call" | custom-call | tf_op jit(solution)/shard_map/layer_backward/pallas_call | solution.py:483
  41.7 0.0 copy-start.2
  41.7 1.9 %copy.14 = bf16[1,128,2048]{2,1,0:T(8,128)(2,1)} copy(bf16[1,128,2048]{2,1,0:T(8,128)(2,1)} %bitcast.12) | data formatting | bytes 1048576
  43.6 0.0 copy-done.2
  43.6 0.0 copy-start.1
  43.6 0.8 %copy.15 = bf16[1,128,2048]{2,1,0:T(8,128)(2,1)} copy(bf16[1,128,2048]{2,1,0:T(8,128)(2,1)S(1)} %bitcast.11) | data formatting | bytes 1048576
  44.4 0.4 copy-done.1
  44.8 0.0 copy-start
  44.8 0.8 %copy.16 = bf16[1,128,2048]{2,1,0:T(8,128)(2,1)} copy(bf16[1,128,2048]{2,1,0:T(8,128)(2,1)S(1)} %bitcast.10) | data formatting | bytes 1048576
  45.6 0.4 copy-done
  46.1 0.8 %copy.17 = f32[1,1,32,4096]{3,2,1,0:T(8,128)} copy(f32[1,1,32,4096]{3,2,1,0:T(8,128)S(1)} %bitcast.9) | data formatting | bytes 1048576
Async XLA Ops:
  41.7 2.0 %copy-start.2 = (bf16[128,2048]{1,0:T(8,128)(2,1)S(1)}, bf16[128,2048]{1,0:T(8,128)(2,1)}, u32[]{:S(2)}) copy-start(bf16[128,2048]{1,0:T(8,128)(2,1)} %get-tuple-element.9) | copy-start | bytes 1572868
  43.6 1.2 %copy-start.1 = (bf16[128,2048]{1,0:T(8,128)(2,1)S(1)}, bf16[128,2048]{1,0:T(8,128)(2,1)}, u32[]{:S(2)}) copy-start(bf16[128,2048]{1,0:T(8,128)(2,1)} %get-tuple-element.10) | copy-start | bytes 1572868
  44.8 1.2 %copy-start = (f32[32,4096]{1,0:T(8,128)S(1)}, f32[32,4096]{1,0:T(8,128)}, u32[]{:S(2)}) copy-start(f32[32,4096]{1,0:T(8,128)} %get-tuple-element.11) | copy-start | bytes 1572868

commit v5 on v4

--- a/solution.py
+++ b/solution.py
@@ -201,8 +201,8 @@
 
 def kernel(
     dh, width, upstream, q, k, v, rates, checkpoint,
-    gq, gk, gv, start,
-    rows_of_heads, stage,
+    gq, gk, gv, rows_of_heads,
+    stage,
     z, trail, err, car, kp, a, b, other_a, other_b, pair_a, pair_b, second_a, second_b,
     entering, leaving, back, end,
     line_sem, up_sems, a_send, a_recv, b_send, b_recv, g_send, g_recv, r_send, r_recv,
@@ -249,13 +249,6 @@
             line_sem.at[i],
         )
 
-    def line_out(i):
-        return pltpu.make_async_copy(
-            rows_of_heads.at[pl.ds(i * heads, heads), :],
-            start.at[:, pl.ds(i * LANES, LANES)],
-            line_sem.at[i],
-        )
-
     for i in range(lines):
         line_in(i).start()
     for i in range(lines):
@@ -307,14 +300,25 @@
     def send_b(i):
         return remote(b.at[:, others(i)], other_b.at[:, place(i)], b_send.at[i], b_recv.at[i], partner)
 
+    def thin(i):
+        return pl.ds(pl.multiple_of(i * LANES, LANES), LANES)
+
+    def own_thin(i):
+        return pl.ds(pl.multiple_of(side * half + i * LANES, LANES), LANES)
+
+    def others_thin(i):
+        return pl.ds(pl.multiple_of((1 - side) * half + i * LANES, LANES), LANES)
+
+    fine = width // LANES
+
     def send_g(i):
-        return remote(leaving.at[:, place(i)], entering.at[:, place(i)], g_send.at[i], g_recv.at[i], before)
+        return remote(leaving.at[:, thin(i)], entering.at[:, thin(i)], g_send.at[i], g_recv.at[i], before)
 
     def send_r(i):
-        return remote(back.at[:, place(i)], end.at[:, own(i)], r_send.at[i], r_recv.at[i], partner)
+        return remote(back.at[:, thin(i)], end.at[:, own_thin(i)], r_send.at[i], r_recv.at[i], partner)
 
     def await_r(i):
-        return remote(back.at[:, place(i)], end.at[:, others(i)], r_send.at[i], r_recv.at[i], partner)
+        return remote(back.at[:, thin(i)], end.at[:, others_thin(i)], r_send.at[i], r_recv.at[i], partner)
 
     def narrow(span):
         start_lane = span.start
@@ -365,12 +369,12 @@
         put(gv, lanes, value_grads)
         store_start(lanes, first)
 
-    def each(body):
+    def each(body, first=0, last=chunks):
         def step(i, nothing):
             body(i)
             return nothing
 
-        lax.fori_loop(0, chunks, step, jnp.int32(0))
+        lax.fori_loop(first, last, step, jnp.int32(0))
 
     def first_step(i):
         for span in (others(i), own(i)):
@@ -400,16 +404,19 @@
 
         @pl.when(not_first & jnp.logical_not(not_last))
         def _():
-            send_g(i).start()
+            for j in range(fine):
+                send_g(i * fine + j).start()
 
         pair_b[:, local] = offset
         pair_a[:, local] = full_times(a0, halves(a1, dh))
         second_a[:, local] = a1
         second_b[:, local] = b1
 
+    def score_step(i):
+        together(scores_of, put_scores, [others(i), own(i)])
+
     def relay_step(i):
-        lanes, local = own(i), place(i)
-        together(scores_of, put_scores, [others(i), lanes])
+        lanes, local = own_thin(i), thin(i)
 
         @pl.when(not_last)
         def _():
@@ -436,30 +443,47 @@
         send_r(i).start()
 
     def last_step(i):
-        await_r(i).wait_recv()
+        for j in range(fine):
+            await_r(i * fine + j).wait_recv()
         together(finals_of, put_finals, [own(i), others(i)])
 
     def drain(i):
         send_a(i).wait_send()
         send_b(i).wait_send()
-        send_r(i).wait_send()
-
-        @pl.when(not_first)
-        def _():
-            send_g(i).wait_send()
+        for j in range(fine):
+            send_r(i * fine + j).wait_send()
+
+            @pl.when(not_first)
+            def _():
+                send_g(i * fine + j).wait_send()
 
     each(first_step)
     upward.wait_recv()
     each(second_step)
     each(pair_step)
-    each(relay_step)
+    early = jnp.where(shard < shards - 4, chunks, 0)
+    each(score_step, 0, early)
+    each(relay_step, 0, chunks * fine)
+    each(score_step, early, chunks)
     each(last_step)
-    for i in range(lines):
-        line_out(i).start()
     each(drain)
     upward.wait_send()
-    for i in range(lines):
-        line_out(i).wait()
+
+
+def store_kernel(heads, gq, gk, gv, rows, gq_out, gk_out, gv_out, start_out, sems, line_sem):
+    copies = [
+        pltpu.make_async_copy(
+            rows.at[pl.ds(i * heads, heads), :], start_out.at[:, pl.ds(i * LANES, LANES)], line_sem.at[i]
+        )
+        for i in range(rows.shape[0] // heads)
+    ] + [
+        pltpu.make_async_copy(x, y, sems.at[i])
+        for i, (x, y) in enumerate(((gq, gq_out), (gk, gk_out), (gv, gv_out)))
+    ]
+    for copy in copies:
+        copy.start()
+    for copy in copies:
+        copy.wait()
 
 
 def per_device(queries, memory_keys, memory_values, upstream, inner_rate, checkpoints):
@@ -477,16 +501,16 @@
     assert 2 * dh == LANES
     lines = dh * dh // LANES
     tall = jax.ShapeDtypeStruct((tokens, features), BF16)
+    held = pltpu.VMEM((tokens, features), BF16)
     whole = pltpu.VMEM((dh, features), F32)
     part = pltpu.VMEM((dh, half), F32)
     rows = pltpu.VMEM((tokens, features), F32)
-    gq, gk, gv, start = pl.pallas_call(
+    gq, gk, gv, start_rows = pl.pallas_call(
         partial(kernel, dh, width),
         in_specs=[hbm] + [vmem] * 3 + [pl.BlockSpec(memory_space=pltpu.SMEM), hbm],
-        out_specs=[vmem] * 3 + [hbm],
-        out_shape=[tall, tall, tall, jax.ShapeDtypeStruct((heads, dh * dh), F32)],
+        out_specs=[vmem] * 4,
+        out_shape=[held, held, held, pltpu.VMEM((lines * heads, LANES), F32)],
         scratch_shapes=[
-            pltpu.VMEM((lines * heads, LANES), F32),
             pltpu.VMEM((features // LANES * dh, LANES), F32),
             pltpu.VMEM((tokens, features), BF16),
             pltpu.VMEM((count * dh, features), F32),
@@ -496,10 +520,20 @@
             whole,
             pltpu.SemaphoreType.DMA((lines,)),
             pltpu.SemaphoreType.DMA((2,)),
-        ] + [pltpu.SemaphoreType.DMA((chunks,))] * 8,
-        compiler_params=pltpu.CompilerParams(collective_id=0, has_side_effects=True),
+        ] + [pltpu.SemaphoreType.DMA((chunks,))] * 4
+        + [pltpu.SemaphoreType.DMA((half // LANES,))] * 4,
+        compiler_params=pltpu.CompilerParams(collective_id=0, has_side_effects=True, vmem_limit_bytes=40 * 2**20),
         name="layer_backward",
     )(upstream[0], queries[0], memory_keys[0], memory_values[0], inner_rate, checkpoints[0, 0])
+    gq, gk, gv, start = pl.pallas_call(
+        partial(store_kernel, heads),
+        in_specs=[hbm] * 4,
+        out_specs=[hbm] * 4,
+        out_shape=[tall, tall, tall, jax.ShapeDtypeStruct((heads, dh * dh), F32)],
+        scratch_shapes=[pltpu.SemaphoreType.DMA((3,)), pltpu.SemaphoreType.DMA((lines,))],
+        compiler_params=pltpu.CompilerParams(vmem_limit_bytes=2**20),
+        name="store_results",
+    )(gq, gk, gv, start_rows)
     return gq[None], gk[None], gv[None], start[None, None]
 
 

time: 47.2 us -> 44.2 us (0.936)
  Pallas kernels: 41 us -> 37.3 us
  local copies, waits for them, and re-layouts: 5.19 us -> 5.85 us
    pallas_call x1, Pallas kernels: 41 us -> 35.7 us  [per_device(): pl.pallas_call(partial(kernel, dh, width), in_specs=[hbm] + [vmem] * 3 +...]
    pallas_call x0 -> x1, Pallas kernels: none -> 1.62 us  [per_device(): pl.pallas_call(partial(store_kernel, heads), in_specs=[hbm] * 4, out_spec...]
    unnamed x10 -> x12, local copies, waits for them, and re-layouts: 5.19 us -> 5.85 us
where the time goes in v5:
time: 44.2 us; the launch traced here: 43.8 us
  Pallas kernels  37.3 us (84%)
  local copies, waits for them, and re-layouts  5.85 us (13%)
  between operations  0.65 us (1%)
    pallas_call x1, Pallas kernels, per_device(): pl.pallas_call(partial(kernel, dh, width), in_specs=[hbm] + [vmem] * 3 +...  35.7 us
    unnamed x12, local copies, waits for them, and re-layouts  5.85 us
    pallas_call x1, Pallas kernels, per_device(): pl.pallas_call(partial(store_kernel, heads), in_specs=[hbm] * 4, out_spec...  1.62 us

profile of v5, /device:TPU:1, one launch (start us, length us, event | category | flops | bytes accessed | tf_op | source)
XLA Modules:
  0.0 43.8 jit_solution(9772547389263846992)
XLA Ops:
  0.6 0.0 copy-start.5
  0.6 0.6 %copy-done.5 = f32[1,32]{1,0:T(1,128)S(1)} copy-done((f32[1,32]{1,0:T(1,128)S(1)}, f32[1,32]{1,0:T(1,128)}, u32[]{:S(2)}) %copy-start.5) | copy-done | bytes 152
  1.3 0.0 copy-start
  1.3 1.0 %copy-done = bf16[1,128,2048]{2,1,0:T(8,128)(2,1)S(1)} copy-done((bf16[1,128,2048]{2,1,0:T(8,128)(2,1)S(1)}, bf16[1,128,2048]{2,1,0:T(8,128)(2,1)}, u32[]{:S(2)}) %copy-start) | copy-done | bytes 524312
  2.3 0.0 copy-start.1
  2.3 1.0 %copy-done.1 = bf16[1,128,2048]{2,1,0:T(8,128)(2,1)S(1)} copy-done((bf16[1,128,2048]{2,1,0:T(8,128)(2,1)S(1)}, bf16[1,128,2048]{2,1,0:T(8,128)(2,1)}, u32[]{:S(2)}) %copy-start.1) | copy-done | bytes 524312
  3.4 0.0 copy-start.2
  3.4 1.0 %copy-done.2 = bf16[1,128,2048]{2,1,0:T(8,128)(2,1)S(1)} copy-done((bf16[1,128,2048]{2,1,0:T(8,128)(2,1)S(1)}, bf16[1,128,2048]{2,1,0:T(8,128)(2,1)}, u32[]{:S(2)}) %copy-start.2) | copy-done | bytes 524312
  4.4 0.0 copy-start.3
  4.4 1.0 %copy-done.3 = bf16[1,128,2048]{2,1,0:T(8,128)(2,1)S(1)} copy-done((bf16[1,128,2048]{2,1,0:T(8,128)(2,1)S(1)}, bf16[1,128,2048]{2,1,0:T(8,128)(2,1)}, u32[]{:S(2)}) %copy-start.3) | copy-done | bytes 524312
  5.5 0.0 copy-start.4
  5.5 1.0 %copy-done.4 = f32[1,1,32,4096]{3,2,1,0:T(8,128)S(1)} copy-done((f32[1,1,32,4096]{3,2,1,0:T(8,128)S(1)}, f32[1,1,32,4096]{3,2,1,0:T(8,128)}, u32[]{:S(2)}) %copy-start.4) | copy-done | bytes 524312
  6.5 35.7 %layer_backward.1 = (bf16[128,2048]{1,0:T(8,128)(2,1)S(1)}, bf16[128,2048]{1,0:T(8,128)(2,1)S(1)}, bf16[128,2048]{1,0:T(8,128)(2,1)S(1)}, f32[1024,128]{1,0:T(8,128)S(1)}) custom-call(bf16[128,2048]{1,0:T(8,128)(2,1)S(1)} %bitcast.9, bf16[128,2048]{1,0:T(8,128)(2,1)S(1)} %bitcast.10, bf16[128,2048]{1,0:T(8,128)(2,1)S(1)} %bitcast.11, ...), custom_call_target="tpu_custom_call" | custom-call | tf_op jit(solution)/shard_map/layer_backward/pallas_call | solution.py:508
  42.2 1.6 %store_results.1 = (bf16[128,2048]{1,0:T(8,128)(2,1)}, bf16[128,2048]{1,0:T(8,128)(2,1)}, bf16[128,2048]{1,0:T(8,128)(2,1)}, f32[32,4096]{1,0:T(8,128)}) custom-call(bf16[128,2048]{1,0:T(8,128)(2,1)S(1)} %get-tuple-element.12.gq, bf16[128,2048]{1,0:T(8,128)(2,1)S(1)} %get-tuple-element.13.gk, bf16[128,2048]{1,0:T(8,128)(2,1)S(1)} %get-tuple-element.14.gv, ...), custom_call_target="tpu_custom_call" | custom-call | tf_op jit(solution)/shard_map/store_results/pallas_call | solution.py:528
Async XLA Ops:
  0.6 0.7 %copy-start.5 = (f32[1,32]{1,0:T(1,128)S(1)}, f32[1,32]{1,0:T(1,128)}, u32[]{:S(2)}) copy-start(f32[1,32]{1,0:T(1,128)} %rates.1) | copy-start | bytes 388
  1.3 1.0 %copy-start = (bf16[1,128,2048]{2,1,0:T(8,128)(2,1)S(1)}, bf16[1,128,2048]{2,1,0:T(8,128)(2,1)}, u32[]{:S(2)}) copy-start(bf16[1,128,2048]{2,1,0:T(8,128)(2,1)} %param.9) | copy-start | bytes 1572868
  2.3 1.0 %copy-start.1 = (bf16[1,128,2048]{2,1,0:T(8,128)(2,1)S(1)}, bf16[1,128,2048]{2,1,0:T(8,128)(2,1)}, u32[]{:S(2)}) copy-start(bf16[1,128,2048]{2,1,0:T(8,128)(2,1)} %param.6) | copy-start | bytes 1572868
  3.4 1.0 %copy-start.2 = (bf16[1,128,2048]{2,1,0:T(8,128)(2,1)S(1)}, bf16[1,128,2048]{2,1,0:T(8,128)(2,1)}, u32[]{:S(2)}) copy-start(bf16[1,128,2048]{2,1,0:T(8,128)(2,1)} %param.7) | copy-start | bytes 1572868
  4.4 1.0 %copy-start.3 = (bf16[1,128,2048]{2,1,0:T(8,128)(2,1)S(1)}, bf16[1,128,2048]{2,1,0:T(8,128)(2,1)}, u32[]{:S(2)}) copy-start(bf16[1,128,2048]{2,1,0:T(8,128)(2,1)} %param.8) | copy-start | bytes 1572868
  5.5 1.0 %copy-start.4 = (f32[1,1,32,4096]{3,2,1,0:T(8,128)S(1)}, f32[1,1,32,4096]{3,2,1,0:T(8,128)}, u32[]{:S(2)}) copy-start(f32[1,1,32,4096]{3,2,1,0:T(8,128)} %param.11) | copy-start | bytes 1572868

commit v6 on v5

--- a/solution.py
+++ b/solution.py
@@ -200,9 +200,9 @@
 
 
 def kernel(
-    dh, width, upstream, q, k, v, rates, checkpoint,
+    dh, width, upstream, q_in, k_in, v_in, rates, checkpoint,
     gq, gk, gv, rows_of_heads,
-    stage,
+    q, k, v, in_sems, stage,
     z, trail, err, car, kp, a, b, other_a, other_b, pair_a, pair_b, second_a, second_b,
     entering, leaving, back, end,
     line_sem, up_sems, a_send, a_recv, b_send, b_recv, g_send, g_recv, r_send, r_recv,
@@ -221,6 +221,13 @@
     not_first = shard >= 2
     not_last = shard < shards - 2
 
+    loads = [
+        pltpu.make_async_copy(x, y, in_sems.at[i])
+        for i, (x, y) in enumerate(((k_in, k), (v_in, v), (q_in, q)))
+    ]
+    for load in loads:
+        load.start()
+
     barrier = pltpu.get_barrier_semaphore()
     for peer in (below, above, partner):
         pl.semaphore_signal(barrier, inc=1, device_id=peer, device_id_type=MESH)
@@ -457,7 +464,10 @@
             def _():
                 send_g(i * fine + j).wait_send()
 
+    loads[0].wait()
+    loads[1].wait()
     each(first_step)
+    loads[2].wait()
     upward.wait_recv()
     each(second_step)
     each(pair_step)
@@ -498,6 +508,7 @@
 
     vmem = pl.BlockSpec(memory_space=pltpu.VMEM)
     hbm = pl.BlockSpec(memory_space=pl.ANY)
+    kept = pl.BlockSpec(memory_space=pltpu.HBM)
     assert 2 * dh == LANES
     lines = dh * dh // LANES
     tall = jax.ShapeDtypeStruct((tokens, features), BF16)
@@ -507,10 +518,10 @@
     rows = pltpu.VMEM((tokens, features), F32)
     gq, gk, gv, start_rows = pl.pallas_call(
         partial(kernel, dh, width),
-        in_specs=[hbm] + [vmem] * 3 + [pl.BlockSpec(memory_space=pltpu.SMEM), hbm],
+        in_specs=[kept] * 4 + [pl.BlockSpec(memory_space=pltpu.SMEM), kept],
         out_specs=[vmem] * 4,
         out_shape=[held, held, held, pltpu.VMEM((lines * heads, LANES), F32)],
-        scratch_shapes=[
+        scratch_shapes=[held, held, held, pltpu.SemaphoreType.DMA((3,))] + [
             pltpu.VMEM((features // LANES * dh, LANES), F32),
             pltpu.VMEM((tokens, features), BF16),
             pltpu.VMEM((count * dh, features), F32),
@@ -522,7 +533,7 @@
             pltpu.SemaphoreType.DMA((2,)),
         ] + [pltpu.SemaphoreType.DMA((chunks,))] * 4
         + [pltpu.SemaphoreType.DMA((half // LANES,))] * 4,
-        compiler_params=pltpu.CompilerParams(collective_id=0, has_side_effects=True, vmem_limit_bytes=40 * 2**20),
+        compiler_params=pltpu.CompilerParams(collective_id=0, has_side_effects=True, vmem_limit_bytes=61 * 2**20 + 2**19),
         name="layer_backward",
     )(upstream[0], queries[0], memory_keys[0], memory_values[0], inner_rate, checkpoints[0, 0])
     gq, gk, gv, start = pl.pallas_call(

time: 44.2 us -> 39.4 us (0.89)
  local copies, waits for them, and re-layouts: 5.85 us -> 0 us
  Pallas kernels: 37.3 us -> 38.4 us
    unnamed x12 -> x0, local copies, waits for them, and re-layouts: 5.85 us -> none
    pallas_call x1, Pallas kernels: 35.7 us -> 36.8 us  [per_device(): pl.pallas_call(partial(kernel, dh, width), in_specs=[kept] * 4 + [pl.Bloc...]
where the time goes in v6:
time: 39.4 us; the launch traced here: 39 us
  Pallas kernels  38.4 us (97%)
  between operations  0.64 us (2%)
    pallas_call x1, Pallas kernels, per_device(): pl.pallas_call(partial(kernel, dh, width), in_specs=[kept] * 4 + [pl.Bloc...  36.8 us
    pallas_call x1, Pallas kernels, per_device(): pl.pallas_call(partial(store_kernel, heads), in_specs=[hbm] * 4, out_spec...  1.62 us

profile of v6, /device:TPU:1, one launch (start us, length us, event | category | flops | bytes accessed | tf_op | source)
XLA Modules:
  0.0 39.0 jit_solution(16943989926758531153)
XLA Ops:
  0.6 36.8 %layer_backward.1 = (bf16[128,2048]{1,0:T(8,128)(2,1)S(1)}, bf16[128,2048]{1,0:T(8,128)(2,1)S(1)}, bf16[128,2048]{1,0:T(8,128)(2,1)S(1)}, f32[1024,128]{1,0:T(8,128)S(1)}) custom-call(bf16[128,2048]{1,0:T(8,128)(2,1)} %bitcast.9, bf16[128,2048]{1,0:T(8,128)(2,1)} %bitcast.10, bf16[128,2048]{1,0:T(8,128)(2,1)} %bitcast.11, bf16[128,2048]{1,0:T(8,128)(2,1)} %bitcast.12, ...), custom_call_target="tpu_custom_call" | custom-call | tf_op jit(solution)/shard_map/layer_backward/pallas_call | solution.py:519
  37.4 1.6 %store_results.1 = (bf16[128,2048]{1,0:T(8,128)(2,1)}, bf16[128,2048]{1,0:T(8,128)(2,1)}, bf16[128,2048]{1,0:T(8,128)(2,1)}, f32[32,4096]{1,0:T(8,128)}) custom-call(bf16[128,2048]{1,0:T(8,128)(2,1)S(1)} %get-tuple-element.12.gq, bf16[128,2048]{1,0:T(8,128)(2,1)S(1)} %get-tuple-element.13.gk, bf16[128,2048]{1,0:T(8,128)(2,1)S(1)} %get-tuple-element.14.gv, ...), custom_call_target="tpu_custom_call" | custom-call | tf_op jit(solution)/shard_map/store_results/pallas_call | solution.py:539
